TPU v7x, 128 devices: a whole 4x4x4 slice. The times are simulated.
128 devices in a mesh: tok: 16 (over x, y), head: 8 (over z, core).
Axes of the slice: x: 4, y: 4, z: 4, core: 2. Of those that a mesh axis runs over, the one named last changes fastest.
Arguments:
- hidden_in: bfloat16 [16384, 2048], P(('tok', 'head')), may hold values from -6 to 6
- attn_gain: float32 [2048], replicated, may hold values from 0.1 to 1.9
- w_qkv: bfloat16 [2048, 2560], P('tok'), may hold values from -0.125 to 0.125
- w_out: bfloat16 [2048, 2048], P('tok'), may hold values from -0.125 to 0.125
- mlp_gain: float32 [2048], replicated, may hold values from 0.1 to 1.9
- w_gate: bfloat16 [2048, 5632], P('tok', 'head'), may hold values from -0.125 to 0.125
- w_up: bfloat16 [2048, 5632], P('tok', 'head'), may hold values from -0.125 to 0.125
- w_down: bfloat16 [5632, 2048], P('head', 'tok'), may hold values from -0.078125 to 0.078125
- cache_kv: bfloat16 [32, 8, 4352, 128], P('tok', 'head'), may hold values from -240 to 240
- cached_len: int32 [32], P('tok'), may hold values from 0 to 8192, as said below
Outputs:
- hidden_out: bfloat16 [16384, 2048], P(('tok', 'head'))
- cache_out: bfloat16 [32, 8, 4352, 128], P('tok', 'head')
Inputs may be any that keep to these rules, and one draw needn't show every extreme that they name: `cached_len`: some request has exactly 8192 cached positions.
All inputs are finite; a program needn't handle non-finite values.
Results may differ from a plain program's by a relative error of at most 0.014.
Values may be sent and summed in bfloat16 or wider, within the bound.
No kernel may reach another device: no remote copies, remote signals or barrier semaphores. Data moves between devices by JAX's collectives and lax.ppermute only.
A program may use at most 128 MiB of HBM per device.

v0:
```python
import jax
import jax.numpy as jnp
from jax import lax
from jax.sharding import PartitionSpec as P

HEADS = 32
KV_HEADS = 4
HEAD_DIM = 64
S_NEW = 512
KEY_BLOCK = 256


ROPE_BASE = 10000.0


def partner_2(array, axis, distance):
    return lax.ppermute(array, axis, [(i, i ^ 1 << distance) for i in range(lax.axis_size(axis))])


def mean_norm(values, gain):
    widened = values.astype(jnp.float32)
    spread = jnp.mean(widened * widened, axis=-1, keepdims=True)
    return (widened * lax.rsqrt(spread + 1e-05) * gain).astype(jnp.bfloat16)


def rotate(values, positions):
    half_dim = values.shape[-1] // 2
    frequency = ROPE_BASE ** (-jnp.arange(half_dim).astype(values.dtype) * 2.0 / values.shape[-1])
    angles = positions[..., None].astype(values.dtype) * frequency
    first_half = values[..., :half_dim]
    second_half = values[..., half_dim:]
    cosine = jnp.cos(angles)
    sine_vals = jnp.sin(angles)
    return jnp.concatenate(
        [
            first_half * cosine - second_half * sine_vals,
            second_half * cosine + first_half * sine_vals,
        ],
        axis=-1,
    )


def lookup(indices, lookup_table):
    matches = indices[:, None] == jnp.arange(lookup_table.shape[0])[None, :]
    return jnp.sum(jnp.where(matches, lookup_table[None, :], 0), axis=1)


def contract(left_rows, shard_rows):
    return jnp.dot(left_rows, shard_rows, preferred_element_type=jnp.float32)


def append_rows(cache_rows, fresh_rows, offset):
    fresh_count = fresh_rows.shape[0]
    slot_count = cache_rows.shape[0]
    padding = jnp.zeros_like(fresh_rows)
    padded = jnp.concatenate([padding, cache_rows, padding], axis=0)
    spot = jnp.clip(offset + fresh_count, 0, slot_count + fresh_count)
    padded = lax.dynamic_update_slice_in_dim(padded, fresh_rows, spot, 0)
    return padded[fresh_count : fresh_count + slot_count]


def attend(query_rows, query_pos, key_values, first_pos, block_count):
    row_count = query_rows.shape[0]
    score_scale = HEAD_DIM ** (-0.5)

    def advance(index, state_carry):
        weighted, row_top, row_total = state_carry
        key_block = lax.dynamic_slice_in_dim(key_values, index * KEY_BLOCK, KEY_BLOCK, 0)
        scores = (
            lax.dot_general(
                query_rows,
                key_block[:, :HEAD_DIM],
                (((1,), (1,)), ((), ())),
                preferred_element_type=jnp.float32,
            )
            * score_scale
        )
        key_pos = first_pos + index * KEY_BLOCK + jnp.arange(KEY_BLOCK)
        scores = jnp.where(key_pos[None, :] <= query_pos[:, None], scores, -jnp.inf)
        new_top = jnp.maximum(row_top, jnp.max(scores, axis=1))
        exps = jnp.exp(scores - new_top[:, None])
        factor = jnp.exp(row_top - new_top)
        row_total = row_total * factor + jnp.sum(exps, axis=1)
        weights = exps.astype(jnp.bfloat16)
        weighted = weighted * factor[:, None] + jnp.dot(
            weights, key_block[:, HEAD_DIM:], preferred_element_type=jnp.float32
        )
        return (weighted, new_top, row_total)

    start_state = (
        jnp.zeros((row_count, HEAD_DIM), jnp.float32),
        jnp.full((row_count,), -1e30, jnp.float32),
        jnp.zeros((row_count,), jnp.float32),
    )
    return lax.fori_loop(0, block_count, advance, start_state)


def per_device(
    hidden_in, attn_gain, w_qkv, w_out, mlp_gain, w_gate, w_up, w_down, cache_kv, cached_len
):
    head_count = lax.axis_size("head")
    head_index = lax.axis_index("head")
    row_count = hidden_in.shape[0]
    group_rows = row_count * head_count
    req_count = cached_len.shape[0]
    heads_dev = HEADS // head_count
    q_width = HEADS * HEAD_DIM
    kv_width = KV_HEADS * HEAD_DIM
    split_count = head_count // KV_HEADS
    part_index = head_index % split_count
    block_pos = cache_kv.shape[2]
    normed = mean_norm(hidden_in, attn_gain)
    group_ids = jnp.arange(group_rows)
    group_pos = lookup(group_ids // S_NEW, cached_len) + group_ids % S_NEW
    projected = contract(normed, lax.all_gather(w_qkv, "tok", axis=0, tiled=True))
    token_ids = head_index * row_count + jnp.arange(row_count)
    token_pos = lookup(token_ids // S_NEW, cached_len) + token_ids % S_NEW
    queries = rotate(
        projected[:, :q_width].reshape(row_count, HEADS, HEAD_DIM), token_pos[:, None]
    ).astype(jnp.bfloat16)
    keys_new = rotate(
        projected[:, q_width : q_width + kv_width].reshape(row_count, KV_HEADS, HEAD_DIM),
        token_pos[:, None],
    ).astype(jnp.bfloat16)
    values_new = (
        projected[:, q_width + kv_width :]
        .reshape(row_count, KV_HEADS, HEAD_DIM)
        .astype(jnp.bfloat16)
    )
    kv_each = jnp.repeat(jnp.concatenate([keys_new, values_new], axis=-1), split_count, axis=1)
    packed = jnp.concatenate(
        [queries.reshape(row_count, head_count, heads_dev * HEAD_DIM), kv_each], axis=-1
    )
    regrouped = lax.all_to_all(packed, "head", split_axis=1, concat_axis=0, tiled=True)
    queries = regrouped[:, 0, : heads_dev * HEAD_DIM].reshape(group_rows, heads_dev, HEAD_DIM)
    new_kv = regrouped[:, 0, heads_dev * HEAD_DIM :]
    new_kv = new_kv.reshape(req_count, S_NEW, 2 * HEAD_DIM)
    own_block = cache_kv[:, 0]
    whole_cache = own_block
    partner = partner_2(whole_cache, "head", 0)
    lower_half = head_index >> 0 & 1 == 0
    whole_cache = jnp.where(
        lower_half,
        jnp.concatenate([whole_cache, partner], axis=1),
        jnp.concatenate([partner, whole_cache], axis=1),
    )
    weighted_list = []
    total_list = []
    for request_idx in range(req_count):
        length = cached_len[request_idx]
        request_cache = append_rows(whole_cache[request_idx], new_kv[request_idx], length)
        whole_cache = whole_cache.at[request_idx].set(request_cache)
        query_rows = (
            queries[request_idx * S_NEW : (request_idx + 1) * S_NEW]
            .transpose(1, 0, 2)
            .reshape(heads_dev * S_NEW, HEAD_DIM)
        )
        query_pos = jnp.tile(group_pos[request_idx * S_NEW : (request_idx + 1) * S_NEW], heads_dev)
        block_count = (length + S_NEW + KEY_BLOCK - 1) // KEY_BLOCK
        weighted, row_top, row_total = attend(query_rows, query_pos, request_cache, 0, block_count)
        weighted_list.append(weighted.reshape(heads_dev, S_NEW, HEAD_DIM))
        total_list.append(row_total.reshape(heads_dev, S_NEW))
    cache_new = lax.dynamic_slice_in_dim(whole_cache, part_index * block_pos, block_pos, 1)[:, None]
    weighted = jnp.concatenate(weighted_list, axis=1)
    row_total = jnp.concatenate(total_list, axis=1)
    attended = (weighted / row_total[..., None]).astype(jnp.bfloat16)
    attended = attended.transpose(1, 0, 2).reshape(group_rows, heads_dev * HEAD_DIM)
    back_rows = lax.all_to_all(attended, "head", split_axis=0, concat_axis=1, tiled=True)
    projected_out = contract(back_rows, lax.all_gather(w_out, "tok", axis=0, tiled=True))
    residual = (hidden_in.astype(jnp.float32) + projected_out).astype(jnp.bfloat16)
    normed2 = mean_norm(residual, mlp_gain)
    gathered2 = lax.all_gather(normed2, "head", axis=0, tiled=True)
    gate_sum = jnp.dot(
        gathered2,
        lax.all_gather(w_gate, "tok", axis=0, tiled=True),
        preferred_element_type=jnp.float32,
    )
    up_sum = jnp.dot(
        gathered2,
        lax.all_gather(w_up, "tok", axis=0, tiled=True),
        preferred_element_type=jnp.float32,
    )
    hidden = (jax.nn.silu(gate_sum) * up_sum).astype(jnp.bfloat16)
    unit_terms = jnp.dot(
        hidden,
        lax.all_gather(w_down, "tok", axis=1, tiled=True),
        preferred_element_type=jnp.float32,
    )
    summed = lax.psum_scatter(
        unit_terms.astype(jnp.bfloat16), "head", scatter_dimension=0, tiled=True
    ).astype(jnp.float32)
    hidden_out = (residual.astype(jnp.float32) + summed).astype(jnp.bfloat16)
    return (hidden_out, cache_new)


def solution(mesh):
    return jax.shard_map(
        per_device,
        mesh=mesh,
        in_specs=(
            P(("tok", "head"), None),
            P(),
            P("tok", None),
            P("tok", None),
            P(),
            P("tok", "head"),
            P("tok", "head"),
            P("head", "tok"),
            P("tok", "head", None, None),
            P("tok"),
        ),
        out_specs=(P(("tok", "head"), None), P("tok", "head", None, None)),
        check_vma=False,
    )
```

profile of v0, /device:TPU:0, one launch (start us, length us, event | category | flops | bytes accessed | tf_op | source)
XLA Modules:
  0.0 569.6 jit_solution(13006370570814280688)
XLA Ops:
  16.3 9.4 %maximum_select_fusion = bf16[2,8704,128]{2,1,0:T(8,128)(2,1)S(1)} fusion(bf16[2,4352,128]{2,1,0:T(8,128)(2,1)S(1)} %collective-permute-done, bf16[2,4352,128]{2,1,0:T(8,128)(2,1)} %bitcast.95, pred[]{:T(512)S(6)} %eq.38), kind=kLoop, calls=%fused_computation.32 | loop fusion | flops 20054016 | bytes 8912897 | tf_op jit(solution)/shard_map/jit(_where)/select_n | solution.py:142
  25.8 2.1 copy-done
  29.3 63.7 %all-gather.7.cloned.1.call-done = bf16[2048,2560]{1,0:T(8,128)(2,1)} async-done(((bf16[128,2560]{1,0:T(8,128)(2,1)}), bf16[2048,2560]{1,0:T(8,128)(2,1)}) %all-gather.7.cloned.1.call-update) | async-done | bytes 10485776 | tf_op jit(solution)/shard_map/all_gather | solution.py:115
  93.0 5.6 fusion.28
  100.4 4.4 all-to-all-start
  104.9 6.5 %pad_maximum_fusion.1 = bf16[9728,128]{1,0:T(8,128)(2,1)S(1)} fusion(bf16[512,128]{1,0:T(8,128)(2,1)S(1)} %broadcast.260, bf16[8704,128]{1,0:T(8,128)(2,1)} %slice_bitcast_fusion.1), kind=kLoop, calls=%fused_computation.35 | loop fusion | flops 7471104 | bytes 4849664 | tf_op jit(solution)/shard_map/concatenate | solution.py:56
  111.3 6.7 %all-to-all-done = bf16[128,8,384]{0,2,1:T(8,128)(2,1)S(1)} async-done(((bf16[128,8,384]{0,2,1:T(8,128)(2,1)}), bf16[128,8,384]{0,2,1:T(8,128)(2,1)S(1)}, u32[]{:S(2)}, u32[]{:S(2)}) %all-to-all-start) | async-done | bytes 786464 | tf_op jit(solution)/shard_map/all_to_all | solution.py:134
  127.1 7.0 %pad_maximum_fusion = bf16[9728,128]{1,0:T(8,128)(2,1)} fusion(bf16[512,128]{1,0:T(8,128)(2,1)S(1)} %broadcast.260, bf16[8704,128]{1,0:T(8,128)(2,1)S(1)} %slice_bitcast_fusion), kind=kLoop, calls=%fused_computation.34 | loop fusion | flops 7471104 | bytes 4849664 | tf_op jit(solution)/shard_map/concatenate | solution.py:56
  134.6 66.0 %while.32 = (s32[]{:T(128)}, f32[2048,64]{0,1:T(8,128)S(1)}, f32[2048]{0:T(1024)S(1)}, f32[2048]{0:T(1024)S(1)}, s32[]{:T(128)}, /*index=5*/bf16[8704,128]{1,0:T...) while((s32[]{:T(128)}, f32[2048,64]{0,1:T(8,128)S(1)}, ...), condition=%wide.region_6.7_spmd.clone, body=%wide.region_3.6_spmd.clone.sunk | while | flops 138678528 | bytes 7901383 | solution.py:95
  200.7 1.8 dynamic_update_slice.7
  202.5 2.7 slice.162
  206.4 40.6 %while.33 = (s32[]{:T(128)}, f32[2048,64]{0,1:T(8,128)S(1)}, f32[2048]{0:T(1024)S(1)}, f32[2048]{0:T(1024)S(1)}, s32[]{:T(128)}, /*index=5*/bf16[8704,128]{1,0:T...) while((s32[]{:T(128)}, f32[2048,64]{0,1:T(8,128)S(1)}, ...), condition=%wide.region_10.11_spmd.clone, body=%wide.region_7.10_spmd.clone.sunk | while | flops 138678528 | bytes 8163527 | solution.py:95
  206.4 1.6 fusion.79
  213.2 1.6 fusion.79
  216.6 1.5 fusion.79
  223.4 1.5 fusion.79
  226.8 1.5 fusion.79
  230.1 1.5 fusion.79
  233.5 1.5 fusion.79
  236.9 1.5 fusion.79
  248.2 3.5 all-to-all-start.1
  252.0 10.0 %all-to-all-done.1 = bf16[8,128,256]{1,2,0:T(8,128)(2,1)S(1)} async-done(((bf16[8,128,256]{1,2,0:T(8,128)(2,1)}), bf16[8,128,256]{1,2,0:T(8,128)(2,1)S(1)}, u32[]{:S(2)}, u32[]{:S(2)}) %all-to-all-start.1) | async-done | bytes 524320 | tf_op jit(solution)/shard_map/all_to_all | solution.py:168
  262.0 4.8 multiply_reduce_fusion
  269.0 136.5 %all-gather.11.cloned.1.call-done = bf16[1024,2048]{1,0:T(8,128)(2,1)} async-done(((bf16[128,2048]{1,0:T(8,128)(2,1)}), bf16[1024,2048]{1,0:T(8,128)(2,1)}) %all-gather.11.cloned.1.call-update) | async-done | bytes 4194320 | tf_op jit(solution)/shard_map/all_gather | solution.py:172
  405.4 7.8 %fusion.50 = f32[1024,704]{0,1:T(8,128)} fusion(bf16[1024,2048]{1,0:T(8,128)(2,1)} %all-gather.11.cloned.1.call-done, bf16[2048,704]{0,1:T(8,128)(2,1)} %all-gather.13.cloned.1.call-done), kind=kOutput, calls=%fused_computation.108 | convolution fusion | flops 2952790016 | bytes 9961472 | tf_op jit(solution)/shard_map/dot_general | solution.py:173
  413.2 45.2 %all-gather.15.cloned.1.call-done = bf16[2048,704]{0,1:T(8,128)(2,1)} async-done(((bf16[128,704]{0,1:T(8,128)(2,1)}), bf16[2048,704]{0,1:T(8,128)(2,1)}) %all-gather.15.cloned.1.call-update) | async-done | bytes 2883600 | tf_op jit(solution)/shard_map/all_gather | solution.py:180
  458.4 52.6 %all-gather.17.cloned.1.call-done = bf16[704,2048]{1,0:T(8,128)(2,1)} async-done(((bf16[704,128]{1,0:T(8,128)(2,1)}), bf16[704,2048]{1,0:T(8,128)(2,1)}) %all-gather.17.cloned.1.call-update) | async-done | bytes 2883600 | tf_op jit(solution)/shard_map/all_gather | solution.py:186
  511.0 12.0 %convolution_convert_fusion = bf16[1024,2048]{1,0:T(8,128)(2,1)} fusion(bf16[704,2048]{1,0:T(8,128)(2,1)} %all-gather.17.cloned.1.call-done, f32[1024,704]{0,1:T(8,128)} %fusion.50, bf16[1024,2048]{1,0:T(8,128)(2,1)} %all-gather.11.cloned.1.call-done, bf16[2048,704]{0,1:T(8,128)(2,1)} %all-gather.15.cloned.1.call-done), kind=kOutput, calls=%fused_computation.33 | convolution fusion | flops 5912002560 | bytes 17039360 | tf_op jit(solution)/shard_map/dot_general | solution.py:184
  523.0 1.7 copy-done.2
  526.2 3.1 dynamic-slice_bitcast_fusion
  529.3 31.5 %reduce-scatter.2.cloned.1.call-done = bf16[128,2048]{1,0:T(8,128)(2,1)} async-done(((bf16[1024,2048]{1,0:T(8,128)(2,1)}), bf16[128,2048]{1,0:T(8,128)(2,1)}) %reduce-scatter.2.cloned.1.call-update) | async-done | bytes 524304 | tf_op jit(solution)/shard_map/reduce_scatter | solution.py:189
  560.8 1.9 add_convert_fusion
  (376 shorter events, 117.0 us)
Async XLA Ops:
  7.2 85.8 %all-gather.7.cloned.1.call-start = ((), (), s32[]{:S(2)}) async-start(), calls=%async_computation.3 | async-start | bytes 11141120 | tf_op jit(solution)/shard_map/all_gather | solution.py:115
  7.9 244.1 %all-gather.9.cloned.1.call-start = ((), (), s32[]{:S(2)}) async-start(), calls=%async_computation.4 | async-start | bytes 8912896 | tf_op jit(solution)/shard_map/all_gather | solution.py:169
  8.6 260.3 %all-gather.13.cloned.1.call-start = ((), (), s32[]{:S(2)}) async-start(), calls=%async_computation.6 | async-start | bytes 3063808 | tf_op jit(solution)/shard_map/all_gather | solution.py:175
  8.7 7.6 %collective-permute-start = (bf16[2,4352,128]{2,1,0:T(8,128)(2,1)}, bf16[2,4352,128]{2,1,0:T(8,128)(2,1)S(1)}, u32[]{:S(2)}, u32[]{:S(2)}) collective-permute-start(bf16[2,4352,128]{2,1,0:T(8,128)(2,1)} %bitcast.94), channel_id=1, source_target_pairs={{0,1},{1,0},{2,3},{3,2},{4,5},{5,4},{6,7},{7,6},{8,9},{9,8},{10,11... | collective-permute-start | bytes 6684680 | tf_op jit(solution)/shard_map/ppermute | solution.py:17
  25.7 2.1 copy-start
  27.8 65.1 %copy-start.3 = (bf16[128,2048]{1,0:T(8,128)(2,1)S(1)}, bf16[128,2048]{1,0:T(8,128)(2,1)}, u32[]{:S(2)}) copy-start(bf16[128,2048]{1,0:T(8,128)(2,1)} %param.18) | copy-start | bytes 1572868
  27.8 65.1 %copy-start.7 = (f32[2048]{0:T(1024)S(1)}, f32[2048]{0:T(1024)}, u32[]{:S(2)}) copy-start(f32[2048]{0:T(1024)} %param.19) | copy-start | bytes 24580
  100.4 17.6 %all-to-all-start = ((bf16[128,8,384]{0,2,1:T(8,128)(2,1)}), bf16[128,8,384]{0,2,1:T(8,128)(2,1)S(1)}, u32[]{:S(2)}, u32[]{:S(2)}) async-start(bf16[128,8,384]{0,2,1:T(8,128)(2,1)} %pad_maximum_fusion.4), calls=%async_computation | async-start | bytes 1572864 | tf_op jit(solution)/shard_map/all_to_all | solution.py:134
  118.0 0.9 copy-start.5
  123.8 3.2 copy-start.1
  200.6 4.5 copy-start.6
  247.1 14.9 %copy-start.4 = (bf16[128,2048]{1,0:T(8,128)(2,1)S(1)}, bf16[128,2048]{1,0:T(8,128)(2,1)}, u32[]{:S(2)}) copy-start(bf16[128,2048]{1,0:T(8,128)(2,1)} %param.18) | copy-start | bytes 1572868
  248.2 13.8 %all-to-all-start.1 = ((bf16[8,128,256]{1,2,0:T(8,128)(2,1)}), bf16[8,128,256]{1,2,0:T(8,128)(2,1)S(1)}, u32[]{:S(2)}, u32[]{:S(2)}) async-start(bf16[8,128,256]{1,2,0:T(8,128)(2,1)} %copy.62), calls=%async_computation.1 | async-start | bytes 1048576 | tf_op jit(solution)/shard_map/all_to_all | solution.py:168
  251.7 153.7 %all-gather.11.cloned.1.call-start = ((), (), s32[]{:S(2)}) async-start(), calls=%async_computation.5 | async-start | bytes 4718592 | tf_op jit(solution)/shard_map/all_gather | solution.py:172
  262.0 4.8 copy-start.8
  267.7 190.7 %all-gather.15.cloned.1.call-start = ((), (), s32[]{:S(2)}) async-start(), calls=%async_computation.7 | async-start | bytes 3063808 | tf_op jit(solution)/shard_map/all_gather | solution.py:180
  268.3 242.7 %all-gather.17.cloned.1.call-start = ((), (), s32[]{:S(2)}) async-start(), calls=%async_computation.8 | async-start | bytes 3063808 | tf_op jit(solution)/shard_map/all_gather | solution.py:186
  268.9 291.9 %reduce-scatter.2.cloned.1.call-start = ((), (), s32[]{:S(2)}) async-start(), calls=%async_computation.9 | async-start | bytes 4718592 | tf_op jit(solution)/shard_map/reduce_scatter | solution.py:189
  523.0 1.7 copy-start.2
Sparse Core Ops, SparseCore 0:
  10.2 82.7 all-gather.6
  95.1 70.3 all-gather.8
  167.6 50.8 all-gather.12
  267.9 137.5 all-gather.10
  407.4 50.9 all-gather.14
  460.4 50.5 all-gather.16
  523.1 37.6 reduce-scatter.1
where the time goes:
time: 576 us; the launch traced here: 570 us
  waiting for transfers between devices  349 us (61%)
  matrix products  123 us (21%)
  other arithmetic  40.8 us (7%)
  local copies, waits for them, and re-layouts  28.4 us (5%)
  between operations  17.1 us (3%)
  starting transfers between devices  8.5 us (1%)
    all_gather x1, waiting for transfers between devices, per_device(): gathered2 = lax.all_gather(normed2, 'head', axis=0, tiled=True)  136 us
    all_gather x1, waiting for transfers between devices, per_device(): lax.all_gather(w_qkv, 'tok', axis=0, tiled=True)  63.7 us
    all_gather x1, waiting for transfers between devices, per_device(): lax.all_gather(w_down, 'tok', axis=1, tiled=True)  52.6 us
    dot_general x33, matrix products, advance(): jnp.dot(weights, key_block[:, HEAD_DIM:], preferred_element_type=jnp.floa...  46.8 us
    dot_general x33, matrix products, advance(): lax.dot_general(query_rows, key_block[:, :HEAD_DIM], (((1,), (1,)), ((),...  46 us
    all_gather x1, waiting for transfers between devices, per_device(): lax.all_gather(w_up, 'tok', axis=0, tiled=True)  45.2 us
    reduce_scatter x1, waiting for transfers between devices, per_device(): lax.psum_scatter(unit_terms.astype(jnp.bfloat16), 'head', scatter_dimensi...  31.5 us
    concatenate x2, other arithmetic, append_rows(): padded = jnp.concatenate([padding, cache_rows, padding], axis=0)  13.5 us
  transfers between devices with their start and end apart: 10, of which 7 were waited for; matrix products, arithmetic and copies ran while one was open for 30% of the time, Pallas kernels for 0%

commit v1 on v0

v1 whole, which is shorter than its diff:
```python
import jax
import jax.numpy as jnp
from jax import lax
from jax.experimental import pallas as pl
from jax.experimental.pallas import tpu as pltpu
from jax.sharding import PartitionSpec as P

HEADS = 32
KV_HEADS = 4
HEAD_DIM = 64
S_NEW = 512
ROPE_BASE = 10000.0

KEYS = 512
ALIGN = 16
WINDOW = S_NEW + ALIGN
VROWS = HEAD_DIM + 16


def mean_norm(values, gain):
    widened = values.astype(jnp.float32)
    spread = jnp.mean(widened * widened, axis=-1, keepdims=True)
    return (widened * lax.rsqrt(spread + 1e-05) * gain).astype(jnp.bfloat16)


def contract(left_rows, right_rows):
    return jnp.dot(left_rows, right_rows, preferred_element_type=jnp.float32)


def attention_kernel(
    lens_ref, part_ref, x_ref, w_ref, cos_ref, sin_ref, own_hbm, other_hbm,
    out_ref, cache_hbm, kv_ref, qt_ref, new_ref, acc_ref, top_ref, load_sems, store_sems,
):
    req_count, block_pos, lanes = own_hbm.shape
    heads_dev = qt_ref.shape[0]
    half = HEAD_DIM // 2
    own_at = pl.multiple_of(part_ref[0] * block_pos, ALIGN)
    other_at = pl.multiple_of((1 - part_ref[0]) * block_pos, ALIGN)

    def loads(r):
        return (
            pltpu.make_async_copy(
                own_hbm.at[r], kv_ref.at[r, pl.ds(own_at, block_pos)], load_sems.at[r, 0]
            ),
            pltpu.make_async_copy(
                other_hbm.at[r], kv_ref.at[r, pl.ds(other_at, block_pos)], load_sems.at[r, 1]
            ),
        )

    def store(r):
        return pltpu.make_async_copy(
            kv_ref.at[r, pl.ds(own_at, block_pos)], cache_hbm.at[r], store_sems.at[r]
        )

    for r in range(req_count):
        for copy in loads(r):
            copy.start()

    cosine = cos_ref[...]
    sine = sin_ref[...]
    x = x_ref[...]

    def turn(block, scale):
        first = block[:half]
        second = block[half:]
        return jnp.concatenate(
            [(first * cosine - second * sine) * scale, (second * cosine + first * sine) * scale],
            axis=0,
        )

    for pair in range(heads_dev // 2):
        flipped = contract(x, w_ref[:, pair * lanes : (pair + 1) * lanes]).T
        for one in range(2):
            rows = turn(flipped[one * HEAD_DIM : (one + 1) * HEAD_DIM], HEAD_DIM**-0.5)
            qt_ref[2 * pair + one] = jnp.concatenate([rows, jnp.zeros_like(rows)], axis=0).astype(
                jnp.bfloat16
            )
    q_lanes = heads_dev * HEAD_DIM
    flipped = contract(x, w_ref[:, q_lanes : q_lanes + lanes]).T
    fresh = jnp.concatenate([turn(flipped[:HEAD_DIM], 1.0), flipped[HEAD_DIM:]], axis=0)
    new_ref[...] = fresh.T.astype(jnp.bfloat16)

    for r in range(req_count):
        length = lens_ref[r]
        for copy in loads(r):
            copy.wait()
        shift = length % ALIGN
        window_at = pl.multiple_of(length - shift, ALIGN)
        row = lax.broadcasted_iota(jnp.int32, (WINDOW, S_NEW), 0)
        col = lax.broadcasted_iota(jnp.int32, (WINDOW, S_NEW), 1)
        pick = (row - shift == col).astype(jnp.float32).astype(jnp.bfloat16)
        moved = contract(pick, new_ref[r * S_NEW : (r + 1) * S_NEW])
        row = lax.broadcasted_iota(jnp.int32, (WINDOW, lanes), 0)
        inside = (row >= shift) & (row < shift + S_NEW)
        old = kv_ref[r, pl.ds(window_at, WINDOW)].astype(jnp.float32)
        kv_ref[r, pl.ds(window_at, WINDOW)] = jnp.where(inside, moved, old).astype(jnp.bfloat16)
        store(r).start()

    for r in range(req_count):
        length = lens_ref[r]

        def step(index, masked, first):
            at = pl.multiple_of(index * KEYS, KEYS)
            block = kv_ref[r, pl.ds(at, KEYS)]
            lane = lax.broadcasted_iota(jnp.int32, (KEYS, lanes), 1)
            ones = jnp.where(lane < HEAD_DIM, 1.0, block.astype(jnp.float32))
            values = ones.T[HEAD_DIM - 16 :].astype(jnp.bfloat16)
            for h in range(heads_dev):
                scores = contract(block, qt_ref[h, :, r * S_NEW : (r + 1) * S_NEW])
                if masked:
                    key = lax.broadcasted_iota(jnp.int32, scores.shape, 0) + (index * KEYS - length)
                    query = lax.broadcasted_iota(jnp.int32, scores.shape, 1)
                    scores = jnp.where(key <= query, scores, -jnp.inf)
                top = jnp.max(scores, axis=0, keepdims=True)
                if not first:
                    old_top = top_ref[h]
                    top = jnp.maximum(top, old_top)
                exps = jnp.exp(scores - top).astype(jnp.bfloat16)
                product = contract(values, exps)
                if not first:
                    product = product + acc_ref[h] * jnp.exp(old_top - top)
                acc_ref[h] = product
                top_ref[h] = top

        tail = length // KEYS
        step(tail, True, True)

        @pl.when(length % KEYS > 0)
        def _():
            step(tail + 1, True, False)

        def full(index, carry):
            step(index, False, False)
            return carry

        lax.fori_loop(0, tail, full, 0)
        for pair in range(heads_dev // 2):
            sides = [
                acc_ref[h][16:] / acc_ref[h][:1] for h in (2 * pair, 2 * pair + 1)
            ]
            out_ref[r * S_NEW : (r + 1) * S_NEW, pair * lanes : (pair + 1) * lanes] = (
                jnp.concatenate(sides, axis=0).T.astype(jnp.bfloat16)
            )

    for r in range(req_count):
        store(r).wait()


def attention(lens, part, x, w, cosine, sine, own, other, interpret=False):
    req_count, block_pos, lanes = own.shape
    rows = x.shape[0]
    heads_dev = (w.shape[1] - lanes) // HEAD_DIM
    whole = pl.BlockSpec(memory_space=pltpu.VMEM)
    scalar = pl.BlockSpec(memory_space=pltpu.SMEM)
    return pl.pallas_call(
        attention_kernel,
        out_shape=(
            jax.ShapeDtypeStruct((rows, heads_dev * HEAD_DIM), jnp.bfloat16),
            jax.ShapeDtypeStruct(own.shape, jnp.bfloat16),
        ),
        in_specs=[
            scalar, scalar, whole, whole, whole, whole,
            pl.BlockSpec(memory_space=pl.ANY), pl.BlockSpec(memory_space=pl.ANY),
        ],
        out_specs=(whole, pl.BlockSpec(memory_space=pl.ANY)),
        scratch_shapes=[
            pltpu.VMEM((req_count, 2 * block_pos + ALIGN, lanes), jnp.bfloat16),
            pltpu.VMEM((heads_dev, lanes, rows), jnp.bfloat16),
            pltpu.VMEM((rows, lanes), jnp.bfloat16),
            pltpu.VMEM((heads_dev, VROWS, S_NEW), jnp.float32),
            pltpu.VMEM((heads_dev, 1, S_NEW), jnp.float32),
            pltpu.SemaphoreType.DMA((req_count, 2)),
            pltpu.SemaphoreType.DMA((req_count,)),
        ],
        compiler_params=pltpu.CompilerParams(vmem_limit_bytes=48 << 20),
        name="attention",
        interpret=interpret,
    )(lens, part, x, w, cosine, sine, own, other)


def angles_of(cached_len):
    half = HEAD_DIM // 2
    frequency = ROPE_BASE ** (-jnp.arange(half).astype(jnp.float32) * 2.0 / HEAD_DIM)
    positions = (cached_len[:, None] + jnp.arange(S_NEW)[None, :]).reshape(-1)
    angles = frequency[:, None] * positions.astype(jnp.float32)[None, :]
    return jnp.cos(angles), jnp.sin(angles)


def per_device(
    hidden_in, attn_gain, w_qkv, w_out, mlp_gain, w_gate, w_up, w_down, cache_kv, cached_len
):
    head_count = lax.axis_size("head")
    head_index = lax.axis_index("head")
    q_width = HEADS * HEAD_DIM
    kv_width = KV_HEADS * HEAD_DIM
    q_dev = q_width // head_count
    split_count = head_count // KV_HEADS
    part_index = head_index % split_count
    kv_head = head_index // split_count

    own = cache_kv[:, 0]
    other = lax.ppermute(own, "head", [(i, i ^ 1) for i in range(head_count)])
    normed = mean_norm(hidden_in, attn_gain)
    group_x = lax.all_gather(normed, "head", axis=0, tiled=True)
    columns = jnp.concatenate(
        [
            lax.dynamic_slice_in_dim(w_qkv, head_index * q_dev, q_dev, 1),
            lax.dynamic_slice_in_dim(w_qkv, q_width + kv_head * HEAD_DIM, HEAD_DIM, 1),
            lax.dynamic_slice_in_dim(w_qkv, q_width + kv_width + kv_head * HEAD_DIM, HEAD_DIM, 1),
        ],
        axis=1,
    )
    group_w = lax.all_gather(columns, "tok", axis=0, tiled=True)
    cosine, sine = angles_of(cached_len)
    attended, cache_new = attention(
        cached_len, part_index.reshape(1), group_x, group_w, cosine, sine, own, other
    )
    back_rows = lax.all_to_all(attended, "head", split_axis=0, concat_axis=1, tiled=True)
    projected_out = contract(back_rows, lax.all_gather(w_out, "tok", axis=0, tiled=True))
    residual = (hidden_in.astype(jnp.float32) + projected_out).astype(jnp.bfloat16)
    normed2 = mean_norm(residual, mlp_gain)
    gathered2 = lax.all_gather(normed2, "head", axis=0, tiled=True)
    gate_sum = contract(gathered2, lax.all_gather(w_gate, "tok", axis=0, tiled=True))
    up_sum = contract(gathered2, lax.all_gather(w_up, "tok", axis=0, tiled=True))
    hidden = (jax.nn.silu(gate_sum) * up_sum).astype(jnp.bfloat16)
    unit_terms = contract(hidden, lax.all_gather(w_down, "tok", axis=1, tiled=True))
    summed = lax.psum_scatter(
        unit_terms.astype(jnp.bfloat16), "head", scatter_dimension=0, tiled=True
    ).astype(jnp.float32)
    hidden_out = (residual.astype(jnp.float32) + summed).astype(jnp.bfloat16)
    return (hidden_out, cache_new[:, None])


def solution(mesh):
    return jax.shard_map(
        per_device,
        mesh=mesh,
        in_specs=(
            P(("tok", "head"), None),
            P(),
            P("tok", None),
            P("tok", None),
            P(),
            P("tok", "head"),
            P("tok", "head"),
            P("head", "tok"),
            P("tok", "head", None, None),
            P("tok"),
        ),
        out_specs=(P(("tok", "head"), None), P("tok", "head", None, None)),
        check_vma=False,
    )
```

time: 576 us -> 415 us (0.72); the launches traced: 570 us -> 415 us
  matrix products: 123 us -> 24.6 us
  Pallas kernels: 0 us -> 54.4 us
  waiting for transfers between devices: 349 us -> 297 us
  other arithmetic: 40.8 us -> 7.51 us
  local copies, waits for them, and re-layouts: 28.4 us -> 3.59 us
  blocking collectives: 0 us -> 13.2 us
  starting transfers between devices: 8.5 us -> 0.62 us
    all_gather x1, waiting for transfers between devices: 136 us -> 33.9 us  [per_device(): gathered2 = lax.all_gather(normed2, 'head', axis=0, tiled=True)]
    dot_general x70 -> x3, matrix products: 123 us -> 24.6 us  [contract(): return jnp.dot(left_rows, right_rows, preferred_element_type=jnp.float32)]
    pallas_call x0 -> x1, Pallas kernels: none -> 54.4 us  [attention(): pl.pallas_call(attention_kernel, out_shape=(jax.ShapeDtypeStruct((rows, h...]
    all_gather x1, waiting for transfers between devices: 0.02 us -> 45.5 us  [per_device(): lax.all_gather(w_gate, 'tok', axis=0, tiled=True)]
    all_to_all x2 -> x0, waiting for transfers between devices: 16.6 us -> none  [the longest x1 9.97 us: per_device(): lax.all_to_all(attended, 'head', split_axis=0, concat_axis=1, tiled=True)]
    concatenate x6 -> x1, other arithmetic: 14.5 us -> 0.73 us  [per_device(): jnp.concatenate([lax.dynamic_slice_in_dim(w_qkv, head_index * q_dev, q_de...]
    all_to_all x0 -> x1, blocking collectives: none -> 13.2 us  [per_device(): lax.all_to_all(attended, 'head', split_axis=0, concat_axis=1, tiled=True)]
    reduce_sum x35 -> x0, other arithmetic: 11.6 us -> none  [the longest x33 10.2 us: advance(): row_total = row_total * factor + jnp.sum(exps, axis=1)]
  transfers between devices with their start and end apart: 10 -> 9, of which waited for: 7 -> 9; matrix products, arithmetic and copies ran while one was open for 30% -> 4% of each run, Pallas kernels for 0% -> 13%
where the time goes in v1:
time: 415 us
  waiting for transfers between devices  297 us (72%)
  Pallas kernels  54.4 us (13%)
  matrix products  24.6 us (6%)
  between operations  14.2 us (3%)
  blocking collectives  13.2 us (3%)
  other arithmetic  7.51 us (2%)
    pallas_call x1, Pallas kernels, attention(): pl.pallas_call(attention_kernel, out_shape=(jax.ShapeDtypeStruct((rows, h...  54.4 us
    all_gather x1, waiting for transfers between devices, per_device(): lax.all_gather(w_down, 'tok', axis=1, tiled=True)  52.8 us
    all_gather x1, waiting for transfers between devices, per_device(): lax.all_gather(w_gate, 'tok', axis=0, tiled=True)  45.5 us
    all_gather x1, waiting for transfers between devices, per_device(): lax.all_gather(w_up, 'tok', axis=0, tiled=True)  45.2 us
    all_gather x1, waiting for transfers between devices, per_device(): group_w = lax.all_gather(columns, 'tok', axis=0, tiled=True)  37.9 us
    reduce_scatter x1, waiting for transfers between devices, per_device(): lax.psum_scatter(unit_terms.astype(jnp.bfloat16), 'head', scatter_dimensi...  37.8 us
    all_gather x1, waiting for transfers between devices, per_device(): group_x = lax.all_gather(normed, 'head', axis=0, tiled=True)  34.1 us
    all_gather x1, waiting for transfers between devices, per_device(): gathered2 = lax.all_gather(normed2, 'head', axis=0, tiled=True)  33.9 us
  transfers between devices with their start and end apart: 9, of which 9 were waited for; matrix products, arithmetic and copies ran while one was open for 4% of the time, Pallas kernels for 13%

profile of v1, /device:TPU:0, one launch (start us, length us, event | category | flops | bytes accessed | tf_op | source)
XLA Modules:
  0.0 414.8 jit_solution(11818741377198489913)
XLA Ops:
  7.3 1.0 constant_dynamic-slice_fusion.2
  8.2 0.9 constant_dynamic-slice_fusion.1
  9.1 0.7 pad_maximum_fusion
  9.9 0.0 all-gather.8.cloned.1.call-start
  9.9 1.2 fusion.2
  11.1 2.0 fusion.4
  13.3 0.7 all-gather.12.cloned.1.call-update
  14.0 0.5 all-gather.16.cloned.1.call-update
  14.6 0.1 collective-permute-start
  14.7 0.1 convert_bitcast_fusion
  14.8 0.5 multiply_sine_fusion
  15.3 3.8 collective-permute-done.other_hbm
  19.1 37.9 %all-gather.10.cloned.1.call-done.w_ref = bf16[2048,384]{1,0:T(8,128)(2,1)} async-done(((bf16[128,384]{1,0:T(8,128)(2,1)}), bf16[2048,384]{1,0:T(8,128)(2,1)}) %all-gather.10.cloned.1.call-update) | async-done | bytes 1572880 | tf_op jit(solution)/shard_map/all_gather | solution.py:213
  57.1 34.1 %all-gather.8.cloned.1.call-done.x_ref = bf16[1024,2048]{1,0:T(8,128)(2,1)} async-done(((bf16[128,2048]{1,0:T(8,128)(2,1)}), bf16[1024,2048]{1,0:T(8,128)(2,1)}) %all-gather.8.cloned.1.call-update) | async-done | bytes 4194320 | tf_op jit(solution)/shard_map/all_gather | solution.py:204
  91.1 1.4 copy-done.1
  92.5 54.4 %attention.1 = (bf16[1024,256]{1,0:T(8,128)(2,1)S(1)}, bf16[2,4352,128]{2,1,0:T(8,128)(2,1)}) custom-call(s32[2]{0:T(128)S(1)} %copy-done.2, s32[1]{0:T(128)} %bitcast.part_ref, bf16[1024,2048]{1,0:T(8,128)(2,1)} %all-gather.8.cloned.1.call-done.x_ref, bf16[2048,384]{1,0:T(8,128)(2,1)S(1)} %copy-done.1, f32[32,1024]{1,0:T(8,128)S(1)} %get-tuple-element.13.cos_ref, ...), custom_call_target="tpu_custom_call" | custom-call | tf_op jit(solution)/shard_map/attention/pallas_call | solution.py:155
  147.0 0.3 copy.13
  147.3 13.2 %all_to_all.19 = bf16[8,128,256]{1,2,0:T(8,128)(2,1)S(1)} all-to-all(bf16[8,128,256]{1,2,0:T(8,128)(2,1)S(1)} %copy.13), channel_id=1, replica_groups=mesh['tok'=16,'head'=8] {'head'}, dimensions={0} | all-to-all | bytes 1048576 | tf_op jit(solution)/shard_map/all_to_all | solution.py:218
  160.4 3.3 all-gather.12.cloned.1.call-done
  163.7 4.8 %multiply_reduce_fusion = (f32[128]{0:T(128)S(1)}, f32[128,2048]{1,0:T(8,128)S(1)}) fusion(bf16[128,2048]{0,1:T(8,128)(2,1)S(1)} %bitcast.22, bf16[2048,2048]{1,0:T(8,128)(2,1)} %all-gather.12.cloned.1.call-done, bf16[128,2048]{1,0:T(8,128)(2,1)S(1)} %copy-done.3), kind=kOutput, calls=%fused_computation.12 | convolution fusion | flops 1075314560 | bytes 10486272 | tf_op jit(solution)/shard_map/dot_general | solution.py:27
  168.5 1.0 multiply_convert_fusion.1
  169.6 0.5 all-gather.18.cloned.1.call-update
  170.1 0.7 all-gather.20.cloned.1.call-update
  170.8 0.3 reduce-scatter.2.cloned.1.call-start
  171.1 45.5 %all-gather.16.cloned.1.call-done = bf16[2048,704]{0,1:T(8,128)(2,1)} async-done(((bf16[128,704]{0,1:T(8,128)(2,1)}), bf16[2048,704]{0,1:T(8,128)(2,1)}) %all-gather.16.cloned.1.call-update) | async-done | bytes 2883600 | tf_op jit(solution)/shard_map/all_gather | solution.py:223
  216.6 33.9 %all-gather.14.cloned.1.call-done = bf16[1024,2048]{1,0:T(8,128)(2,1)} async-done(((bf16[128,2048]{1,0:T(8,128)(2,1)}), bf16[1024,2048]{1,0:T(8,128)(2,1)}) %all-gather.14.cloned.1.call-update) | async-done | bytes 4194320 | tf_op jit(solution)/shard_map/all_gather | solution.py:222
  250.6 7.8 %fusion.6 = f32[1024,704]{0,1:T(8,128)} fusion(bf16[1024,2048]{1,0:T(8,128)(2,1)} %all-gather.14.cloned.1.call-done, bf16[2048,704]{0,1:T(8,128)(2,1)} %all-gather.16.cloned.1.call-done), kind=kOutput, calls=%fused_computation.24 | convolution fusion | flops 2952790016 | bytes 9961472 | tf_op jit(solution)/shard_map/dot_general | solution.py:27
  258.4 45.2 %all-gather.18.cloned.1.call-done = bf16[2048,704]{0,1:T(8,128)(2,1)} async-done(((bf16[128,704]{0,1:T(8,128)(2,1)}), bf16[2048,704]{0,1:T(8,128)(2,1)}) %all-gather.18.cloned.1.call-update) | async-done | bytes 2883600 | tf_op jit(solution)/shard_map/all_gather | solution.py:224
  303.6 52.8 %all-gather.20.cloned.1.call-done = bf16[704,2048]{1,0:T(8,128)(2,1)} async-done(((bf16[704,128]{1,0:T(8,128)(2,1)}), bf16[704,2048]{1,0:T(8,128)(2,1)}) %all-gather.20.cloned.1.call-update) | async-done | bytes 2883600 | tf_op jit(solution)/shard_map/all_gather | solution.py:226
  356.3 12.0 %convolution_convert_fusion = bf16[1024,2048]{1,0:T(8,128)(2,1)} fusion(bf16[704,2048]{1,0:T(8,128)(2,1)} %all-gather.20.cloned.1.call-done, f32[1024,704]{0,1:T(8,128)} %fusion.6, bf16[1024,2048]{1,0:T(8,128)(2,1)} %all-gather.14.cloned.1.call-done, bf16[2048,704]{0,1:T(8,128)(2,1)} %all-gather.18.cloned.1.call-done), kind=kOutput, calls=%fused_computation | convolution fusion | flops 5912002560 | bytes 17039360 | tf_op jit(solution)/shard_map/dot_general | solution.py:27
  368.3 37.8 %reduce-scatter.2.cloned.1.call-done = bf16[128,2048]{1,0:T(8,128)(2,1)} async-done(((bf16[1024,2048]{1,0:T(8,128)(2,1)}), bf16[128,2048]{1,0:T(8,128)(2,1)}) %reduce-scatter.2.cloned.1.call-update) | async-done | bytes 524304 | tf_op jit(solution)/shard_map/reduce_scatter | solution.py:227
  406.1 1.9 add_convert_fusion
  (23 shorter events, 0.3 us)
Async XLA Ops:
  7.2 7.4 %copy-start = (bf16[2,1,4352,128]{3,2,1,0:T(8,128)(2,1)S(1)}, bf16[2,1,4352,128]{3,2,1,0:T(8,128)(2,1)}, u32[]{:S(2)}) copy-start(bf16[2,1,4352,128]{3,2,1,0:T(8,128)(2,1)} %param.18) | copy-start | bytes 6684676
  7.2 7.5 %copy-start.2 = (s32[2]{0:T(128)S(1)}, s32[2]{0:T(128)}, u32[]{:S(2)}) copy-start(s32[2]{0:T(128)} %lens_ref.1) | copy-start | bytes 28
  7.2 49.9 %all-gather.10.cloned.1.call-start = ((), (), s32[]{:S(2)}) async-start(), calls=%async_computation.3 | async-start | bytes 1671168 | tf_op jit(solution)/shard_map/all_gather | solution.py:213
  9.9 81.3 %all-gather.8.cloned.1.call-start = ((), (), s32[]{:S(2)}) async-start(), calls=%async_computation.2 | async-start | bytes 4718592 | tf_op jit(solution)/shard_map/all_gather | solution.py:204
  13.2 150.5 %all-gather.12.cloned.1.call-start = ((), (), s32[]{:S(2)}) async-start(), calls=%async_computation.4 | async-start | bytes 8912896 | tf_op jit(solution)/shard_map/all_gather | solution.py:219
  13.9 202.7 %all-gather.16.cloned.1.call-start = ((), (), s32[]{:S(2)}) async-start(), calls=%async_computation.6 | async-start | bytes 3063808 | tf_op jit(solution)/shard_map/all_gather | solution.py:223
  14.5 236.0 %all-gather.14.cloned.1.call-start = ((), (), s32[]{:S(2)}) async-start(), calls=%async_computation.5 | async-start | bytes 4718592 | tf_op jit(solution)/shard_map/all_gather | solution.py:222
  14.6 4.6 %collective-permute-start = (bf16[2,4352,128]{2,1,0:T(8,128)(2,1)S(1)}, bf16[2,4352,128]{2,1,0:T(8,128)(2,1)}, u32[]{:S(2)}, u32[]{:S(2)}) collective-permute-start(bf16[2,4352,128]{2,1,0:T(8,128)(2,1)S(1)} %bitcast.19), channel_id=1, source_target_pairs={{0,1},{1,0},{2,3},{3,2},{4,5},{5,4},{6,7},{7,6},{8,9},{9,8},{10,11... | collective-permute-start | bytes 6684680 | tf_op jit(solution)/shard_map/ppermute | solution.py:202
  91.1 1.4 copy-start.1
  92.5 71.2 %copy-start.3 = (bf16[128,2048]{1,0:T(8,128)(2,1)S(1)}, bf16[128,2048]{1,0:T(8,128)(2,1)}, u32[]{:S(2)}) copy-start(bf16[128,2048]{1,0:T(8,128)(2,1)} %param.10) | copy-start | bytes 1572868
  163.7 4.8 %copy-start.4 = (f32[2048]{0:T(1024)S(1)}, f32[2048]{0:T(1024)}, u32[]{:S(2)}) copy-start(f32[2048]{0:T(1024)} %param.14) | copy-start | bytes 24580
  169.5 134.0 %all-gather.18.cloned.1.call-start = ((), (), s32[]{:S(2)}) async-start(), calls=%async_computation.7 | async-start | bytes 3063808 | tf_op jit(solution)/shard_map/all_gather | solution.py:224
  170.1 186.2 %all-gather.20.cloned.1.call-start = ((), (), s32[]{:S(2)}) async-start(), calls=%async_computation.8 | async-start | bytes 3063808 | tf_op jit(solution)/shard_map/all_gather | solution.py:226
  170.8 235.2 %reduce-scatter.2.cloned.1.call-start = ((), (), s32[]{:S(2)}) async-start(), calls=%async_computation.9 | async-start | bytes 4718592 | tf_op jit(solution)/shard_map/reduce_scatter | solution.py:227
Sparse Core Ops, SparseCore 0:
  10.8 46.2 all-gather.9
  59.4 31.7 all-gather.7
  93.3 70.4 all-gather.11
  165.7 50.8 all-gather.15
  218.8 31.7 all-gather.13
  252.5 50.9 all-gather.17
  305.7 50.5 all-gather.19
  368.4 37.5 reduce-scatter.1

commit v2 on v1

v2 whole, which is shorter than its diff:
```python
import jax
import jax.numpy as jnp
from jax import lax
from jax.experimental import pallas as pl
from jax.experimental.pallas import tpu as pltpu
from jax.sharding import PartitionSpec as P

HEADS = 32
KV_HEADS = 4
HEAD_DIM = 64
S_NEW = 512
ROPE_BASE = 10000.0

KEYS = 512
ALIGN = 16
WINDOW = S_NEW + ALIGN
VROWS = HEAD_DIM + 16


Z = 4
FF_PAIR = 128


def mean_norm(values, gain):
    widened = values.astype(jnp.float32)
    spread = jnp.mean(widened * widened, axis=-1, keepdims=True)
    return (widened * lax.rsqrt(spread + 1e-05) * gain).astype(jnp.bfloat16)


def contract(left_rows, right_rows):
    return jnp.dot(left_rows, right_rows, preferred_element_type=jnp.float32)


def exchange(array):
    return lax.ppermute(array, "head", [(i, i ^ 1) for i in range(lax.axis_size("head"))])


def along_z(array, distance):
    count = lax.axis_size("head")
    return lax.ppermute(array, "head", [(i, (i + 2 * distance) % count) for i in range(count)])


def along_tok(array, distance, major):
    moves = []
    for i in range(lax.axis_size("tok")):
        x, y = i // Z, i % Z
        moves.append((i, (x + distance) % Z * Z + y if major else x * Z + (y + distance) % Z))
    return lax.ppermute(array, "tok", moves)


def gather_head(array):
    same_core = [array] + [along_z(array, d) for d in range(1, Z)]
    return same_core + [exchange(piece) for piece in same_core]


def sources():
    head_index = lax.axis_index("head")
    z, core = head_index // 2, head_index % 2
    chips = (z - jnp.arange(Z)) % Z * 2
    return jnp.concatenate([chips + core, chips + 1 - core]).astype(jnp.int32)


def attend(length, kv_ref, qt_ref, acc_ref, top_ref, out_ref):
    heads_dev = qt_ref.shape[0]
    lanes = kv_ref.shape[1]

    def step(index, masked, first):
        at = pl.multiple_of(index * KEYS, KEYS)
        block = kv_ref[pl.ds(at, KEYS)]
        lane = lax.broadcasted_iota(jnp.int32, (KEYS, lanes), 1)
        ones = jnp.where(lane < HEAD_DIM, 1.0, block.astype(jnp.float32))
        values = ones.T[HEAD_DIM - 16 :].astype(jnp.bfloat16)
        for h in range(heads_dev):
            scores = contract(block, qt_ref[h])
            if masked:
                key = lax.broadcasted_iota(jnp.int32, scores.shape, 0) + (index * KEYS - length)
                query = lax.broadcasted_iota(jnp.int32, scores.shape, 1)
                scores = jnp.where(key <= query, scores, -jnp.inf)
            top = jnp.max(scores, axis=0, keepdims=True)
            if not first:
                old_top = top_ref[h]
                top = jnp.maximum(top, old_top)
            exps = jnp.exp(scores - top).astype(jnp.bfloat16)
            product = contract(values, exps)
            if not first:
                product = product + acc_ref[h] * jnp.exp(old_top - top)
            acc_ref[h] = product
            top_ref[h] = top

    tail = length // KEYS
    step(tail, True, True)

    @pl.when(length % KEYS > 0)
    def _():
        step(tail + 1, True, False)

    def full(index, carry):
        step(index, False, False)
        return carry

    lax.fori_loop(0, tail, full, 0)
    for pair in range(heads_dev // 2):
        sides = [acc_ref[h][16:] / acc_ref[h][:1] for h in (2 * pair, 2 * pair + 1)]
        out_ref[:, pair * lanes : (pair + 1) * lanes] = (
            jnp.concatenate(sides, axis=0).T.astype(jnp.bfloat16)
        )


def first_kernel(
    lens_ref, part_ref, src_ref, tok_ref, gain_ref, cos_ref, sin_ref, *refs
):
    x_pieces = refs[: 2 * Z]
    w_pieces = refs[2 * Z : 3 * Z]
    own_hbm, other_hbm = refs[3 * Z : 3 * Z + 2]
    out_ref, later_qt_ref, later_kv_hbm, cache_hbm, rows_hbm = refs[3 * Z + 2 : 3 * Z + 7]
    x_ref, w_ref, kv_ref, qt_ref, new_ref, acc_ref, top_ref = refs[3 * Z + 7 : 3 * Z + 14]
    x_sems, w_sems, load_sems, store_sems = refs[3 * Z + 14 :]
    req_count, block_pos, lanes = own_hbm.shape
    heads_dev = qt_ref.shape[0]
    half = HEAD_DIM // 2
    piece_rows = x_pieces[0].shape[0]
    own_at = pl.multiple_of(part_ref[0] * block_pos, ALIGN)
    other_at = pl.multiple_of((1 - part_ref[0]) * block_pos, ALIGN)

    def x_load(i):
        at = pl.multiple_of(src_ref[i] * piece_rows, piece_rows)
        return pltpu.make_async_copy(x_pieces[i], x_ref.at[pl.ds(at, piece_rows)], x_sems.at[i])

    def w_load(i, j):
        rows = w_pieces[0].shape[1]
        at = pl.multiple_of(tok_ref[i * Z + j] * rows, rows)
        return pltpu.make_async_copy(
            w_pieces[i].at[j], w_ref.at[pl.ds(at, rows)], w_sems.at[i * Z + j]
        )

    def loads(r):
        return (
            pltpu.make_async_copy(
                own_hbm.at[r], kv_ref.at[r, pl.ds(own_at, block_pos)], load_sems.at[r, 0]
            ),
            pltpu.make_async_copy(
                other_hbm.at[r], kv_ref.at[r, pl.ds(other_at, block_pos)], load_sems.at[r, 1]
            ),
        )

    def stores(r):
        copies = [
            pltpu.make_async_copy(
                kv_ref.at[r, pl.ds(own_at, block_pos)], cache_hbm.at[r], store_sems.at[r]
            )
        ]
        if r:
            copies.append(pltpu.make_async_copy(kv_ref.at[r], later_kv_hbm, store_sems.at[2]))
        return copies

    for i in range(2 * Z):
        x_load(i).start()
    for i in range(Z):
        for j in range(Z):
            w_load(i, j).start()
    for r in range(req_count):
        for copy in loads(r):
            copy.start()
    for i in range(2 * Z):
        x_load(i).wait()
    keep = pltpu.make_async_copy(x_ref, rows_hbm, store_sems.at[3])
    keep.start()
    for i in range(Z):
        for j in range(Z):
            w_load(i, j).wait()

    q_lanes = heads_dev * HEAD_DIM
    gain = gain_ref[...]
    for r in range(req_count):
        here = slice(r * S_NEW, (r + 1) * S_NEW)
        cosine = cos_ref[:, here]
        sine = sin_ref[:, here]

        def turn(block, scale):
            first = block[:half]
            second = block[half:]
            return jnp.concatenate(
                [
                    (first * cosine - second * sine) * scale,
                    (second * cosine + first * sine) * scale,
                ],
                axis=0,
            )

        normed = mean_norm(x_ref[here], gain)
        projected = contract(normed, w_ref[...])
        for pair in range(heads_dev // 2):
            flipped = projected[:, pair * lanes : (pair + 1) * lanes].T
            for one in range(2):
                rows = turn(flipped[one * HEAD_DIM : (one + 1) * HEAD_DIM], HEAD_DIM**-0.5)
                rows = jnp.concatenate([rows, jnp.zeros_like(rows)], axis=0).astype(jnp.bfloat16)
                if r:
                    later_qt_ref[2 * pair + one] = rows
                else:
                    qt_ref[2 * pair + one] = rows
        flipped = projected[:, q_lanes:].T
        fresh = jnp.concatenate([turn(flipped[:HEAD_DIM], 1.0), flipped[HEAD_DIM:]], axis=0)
        new_ref[r] = fresh.T.astype(jnp.bfloat16)

    for r in range(req_count):
        length = lens_ref[r]
        for copy in loads(r):
            copy.wait()
        shift = length % ALIGN
        window_at = pl.multiple_of(length - shift, ALIGN)
        row = lax.broadcasted_iota(jnp.int32, (WINDOW, S_NEW), 0)
        col = lax.broadcasted_iota(jnp.int32, (WINDOW, S_NEW), 1)
        pick = (row - shift == col).astype(jnp.float32).astype(jnp.bfloat16)
        moved = contract(pick, new_ref[r])
        row = lax.broadcasted_iota(jnp.int32, (WINDOW, lanes), 0)
        inside = (row >= shift) & (row < shift + S_NEW)
        old = kv_ref[r, pl.ds(window_at, WINDOW)].astype(jnp.float32)
        kv_ref[r, pl.ds(window_at, WINDOW)] = jnp.where(inside, moved, old).astype(jnp.bfloat16)
        for copy in stores(r):
            copy.start()

    attend(lens_ref[0], kv_ref.at[0], qt_ref, acc_ref, top_ref, out_ref)
    for r in range(req_count):
        for copy in stores(r):
            copy.wait()
    keep.wait()


def attend_first(lens, part, src, tok_order, gain, cosine, sine, x_pieces, w_pieces, own, other):
    req_count, block_pos, lanes = own.shape
    piece_rows, width = x_pieces[0].shape
    rows = piece_rows * len(x_pieces)
    w_rows = w_pieces[0].shape[0] * w_pieces[0].shape[1] * len(w_pieces)
    w_cols = w_pieces[0].shape[2]
    heads_dev = (w_cols - lanes) // HEAD_DIM
    positions = 2 * block_pos + ALIGN
    whole = pl.BlockSpec(memory_space=pltpu.VMEM)
    scalar = pl.BlockSpec(memory_space=pltpu.SMEM)
    remote = pl.BlockSpec(memory_space=pl.ANY)
    return pl.pallas_call(
        first_kernel,
        out_shape=(
            jax.ShapeDtypeStruct((S_NEW, heads_dev * HEAD_DIM), jnp.bfloat16),
            jax.ShapeDtypeStruct((heads_dev, lanes, S_NEW), jnp.bfloat16),
            jax.ShapeDtypeStruct((positions, lanes), jnp.bfloat16),
            jax.ShapeDtypeStruct(own.shape, jnp.bfloat16),
            jax.ShapeDtypeStruct((rows, width), jnp.bfloat16),
        ),
        in_specs=[scalar] * 4 + [whole] * 3 + [remote] * (len(x_pieces) + len(w_pieces) + 2),
        out_specs=(whole, whole, remote, remote, remote),
        scratch_shapes=[
            pltpu.VMEM((rows, width), jnp.bfloat16),
            pltpu.VMEM((w_rows, w_cols), jnp.bfloat16),
            pltpu.VMEM((req_count, positions, lanes), jnp.bfloat16),
            pltpu.VMEM((heads_dev, lanes, S_NEW), jnp.bfloat16),
            pltpu.VMEM((req_count, S_NEW, lanes), jnp.bfloat16),
            pltpu.VMEM((heads_dev, VROWS, S_NEW), jnp.float32),
            pltpu.VMEM((heads_dev, 1, S_NEW), jnp.float32),
            pltpu.SemaphoreType.DMA((2 * Z,)),
            pltpu.SemaphoreType.DMA((Z * Z,)),
            pltpu.SemaphoreType.DMA((req_count, 2)),
            pltpu.SemaphoreType.DMA((4,)),
        ],
        compiler_params=pltpu.CompilerParams(vmem_limit_bytes=56 << 20),
        cost_estimate=pl.CostEstimate(
            flops=10**10, transcendentals=10**8, bytes_accessed=40 * 10**6
        ),
        name="attend_first",
    )(lens, part, src, tok_order, gain, cosine, sine, *x_pieces, *w_pieces, own, other)


def second_kernel(len_ref, qt_ref, kv_ref, out_ref, acc_ref, top_ref):
    attend(len_ref[1], kv_ref, qt_ref, acc_ref, top_ref, out_ref)


def attend_second(lens, qt, kv):
    heads_dev = qt.shape[0]
    whole = pl.BlockSpec(memory_space=pltpu.VMEM)
    return pl.pallas_call(
        second_kernel,
        out_shape=jax.ShapeDtypeStruct((S_NEW, heads_dev * HEAD_DIM), jnp.bfloat16),
        in_specs=[pl.BlockSpec(memory_space=pltpu.SMEM), whole, whole],
        out_specs=whole,
        scratch_shapes=[
            pltpu.VMEM((heads_dev, VROWS, S_NEW), jnp.float32),
            pltpu.VMEM((heads_dev, 1, S_NEW), jnp.float32),
        ],
        compiler_params=pltpu.CompilerParams(vmem_limit_bytes=40 << 20),
        cost_estimate=pl.CostEstimate(
            flops=10**10, transcendentals=10**8, bytes_accessed=40 * 10**6
        ),
        name="attend_second",
    )(lens, qt, kv)


def out_kernel(src_ref, gain_ref, w_ref, rows_ref, *refs):
    pieces = refs[: 2 * Z]
    residual_ref, normed_ref, att_ref, sems = refs[2 * Z :]
    index = pl.program_id(0)
    tile = w_ref.shape[1]

    @pl.when(index == 0)
    def _():
        copies = [
            pltpu.make_async_copy(pieces[i], att_ref.at[src_ref[i]], sems.at[i])
            for i in range(2 * Z)
        ]
        for copy in copies:
            copy.start()
        for copy in copies:
            copy.wait()

    attended = jnp.concatenate([att_ref[i] for i in range(2 * Z)], axis=1)
    total = rows_ref[...].astype(jnp.float32) + contract(attended, w_ref[...])
    for i in range(residual_ref.shape[1] // tile):

        @pl.when(index == i)
        def _():
            residual_ref[:, i * tile : (i + 1) * tile] = total.astype(jnp.bfloat16)

    @pl.when(index == pl.num_programs(0) - 1)
    def _():
        normed_ref[...] = mean_norm(residual_ref[...], gain_ref[...])


def project_out(src, gain, weights, rows, pieces, request):
    piece_rows, piece_width = pieces[0].shape
    width = rows.shape[1]
    tile = 512
    remote = pl.BlockSpec(memory_space=pl.ANY)
    return pl.pallas_call(
        out_kernel,
        grid=(width // tile,),
        out_shape=(jax.ShapeDtypeStruct((piece_rows, width), jnp.bfloat16),) * 2,
        in_specs=[
            pl.BlockSpec(memory_space=pltpu.SMEM),
            pl.BlockSpec((1, width), lambda i: (0, 0)),
            pl.BlockSpec((width, tile), lambda i: (0, i)),
            pl.BlockSpec((piece_rows, tile), lambda i: (request, i)),
        ]
        + [remote] * len(pieces),
        out_specs=(pl.BlockSpec((piece_rows, width), lambda i: (0, 0)),) * 2,
        scratch_shapes=[
            pltpu.VMEM((2 * Z, piece_rows, piece_width), jnp.bfloat16),
            pltpu.SemaphoreType.DMA((2 * Z,)),
        ],
        compiler_params=pltpu.CompilerParams(vmem_limit_bytes=40 << 20),
        cost_estimate=pl.CostEstimate(
            flops=4 * 10**9, transcendentals=0, bytes_accessed=20 * 10**6
        ),
        name="project_out",
    )(src, gain, weights, rows, *pieces)


def ff_kernel(core_ref, low_hbm, high_hbm, w_hbm, mine_ref, theirs_ref, x_ref, up_ref, down_ref,
              hidden_ref, x_sems, up_sems, down_sem, chunk, col_at, units):
    tiles = up_ref.shape[0]
    width = x_ref.shape[2]
    count = low_hbm.shape[0]
    rows = x_ref.shape[1]
    x_loads = [
        pltpu.make_async_copy(
            part.at[:, pl.ds(chunk * rows, rows)], x_ref.at[pl.ds(i * count, count)], x_sems.at[i]
        )
        for i, part in enumerate((low_hbm, high_hbm))
    ]
    up_loads = []
    for i in range(tiles):
        cols = min(2 * FF_PAIR, 2 * units - 2 * FF_PAIR * i)
        up_loads.append(
            pltpu.make_async_copy(
                w_hbm.at[:, pl.ds(col_at + 2 * FF_PAIR * i, cols)],
                up_ref.at[i, :, pl.ds(0, cols)],
                up_sems.at[i],
            )
        )
    down_load = pltpu.make_async_copy(
        w_hbm.at[:, pl.ds(col_at + 2 * units, units)], down_ref, down_sem
    )
    for copy in (*x_loads, *up_loads, down_load):
        copy.start()
    for copy in x_loads:
        copy.wait()
    x = x_ref[...].reshape(2 * count * rows, width)
    for i in range(tiles):
        size = min(FF_PAIR, units - FF_PAIR * i)
        up_loads[i].wait()
        both = contract(x, up_ref[i, :, : 2 * size])
        hidden_ref[:, i * FF_PAIR : i * FF_PAIR + size] = (
            jax.nn.silu(both[:, :size]) * both[:, size:]
        ).astype(jnp.bfloat16)
    down_load.wait()
    terms = lax.dot_general(
        hidden_ref[...], down_ref[...], (((1,), (1,)), ((), ())),
        preferred_element_type=jnp.float32,
    ).astype(jnp.bfloat16)
    terms = terms.reshape(Z, 2, rows, width)
    for core in range(2):

        @pl.when(core_ref[0] == core)
        def _():
            mine_ref[...] = terms[:, core]
            theirs_ref[...] = terms[:, 1 - core]


def feed_forward(core, low, high, weights, chunk, col_at, units):
    count, group_rows, width = low.shape
    rows = group_rows // 2
    tiles = -(-units // FF_PAIR)
    whole = pl.BlockSpec(memory_space=pltpu.VMEM)
    remote = pl.BlockSpec(memory_space=pl.ANY)

    def kernel(*refs):
        ff_kernel(*refs, chunk, col_at, units)

    return pl.pallas_call(
        kernel,
        out_shape=(jax.ShapeDtypeStruct((Z, rows, width), jnp.bfloat16),) * 2,
        in_specs=[pl.BlockSpec(memory_space=pltpu.SMEM), remote, remote, remote],
        out_specs=(whole, whole),
        scratch_shapes=[
            pltpu.VMEM((2 * count, rows, width), jnp.bfloat16),
            pltpu.VMEM((tiles, width, 2 * FF_PAIR), jnp.bfloat16),
            pltpu.VMEM((width, units), jnp.bfloat16),
            pltpu.VMEM((2 * count * rows, units), jnp.bfloat16),
            pltpu.SemaphoreType.DMA((2,)),
            pltpu.SemaphoreType.DMA((tiles,)),
            pltpu.SemaphoreType.DMA,
        ],
        compiler_params=pltpu.CompilerParams(vmem_limit_bytes=48 << 20),
        cost_estimate=pl.CostEstimate(
            flops=5 * 10**9, transcendentals=10**6, bytes_accessed=16 * 10**6
        ),
        name="feed_forward",
    )(core, low, high, weights)


def angles_of(cached_len):
    half = HEAD_DIM // 2
    frequency = ROPE_BASE ** (-jnp.arange(half).astype(jnp.float32) * 2.0 / HEAD_DIM)
    positions = (cached_len[:, None] + jnp.arange(S_NEW)[None, :]).reshape(-1)
    angles = frequency[:, None] * positions.astype(jnp.float32)[None, :]
    return jnp.cos(angles), jnp.sin(angles)


def beside(gate, up):
    blocks = []
    for at in range(0, gate.shape[1], FF_PAIR):
        blocks += [gate[:, at : at + FF_PAIR], up[:, at : at + FF_PAIR]]
    return jnp.concatenate(blocks, axis=1)


def per_device(
    hidden_in, attn_gain, w_qkv, w_out, mlp_gain, w_gate, w_up, w_down, cache_kv, cached_len
):
    head_count = lax.axis_size("head")
    head_index = lax.axis_index("head")
    tok_index = lax.axis_index("tok")
    q_width = HEADS * HEAD_DIM
    kv_width = KV_HEADS * HEAD_DIM
    q_dev = q_width // head_count
    split_count = head_count // KV_HEADS
    part_index = head_index % split_count
    kv_head = head_index // split_count
    units = w_gate.shape[1]
    row_count, width = hidden_in.shape

    x_pieces = gather_head(hidden_in)
    columns = jnp.concatenate(
        [
            lax.dynamic_slice_in_dim(w_qkv, head_index * q_dev, q_dev, 1),
            lax.dynamic_slice_in_dim(w_qkv, q_width + kv_head * HEAD_DIM, HEAD_DIM, 1),
            lax.dynamic_slice_in_dim(w_qkv, q_width + kv_width + kv_head * HEAD_DIM, HEAD_DIM, 1),
        ],
        axis=1,
    )
    column = jnp.stack([columns] + [along_tok(columns, d, False) for d in range(1, Z)])
    w_pieces = [column] + [along_tok(column, d, True) for d in range(1, Z)]
    steps = jnp.arange(Z)
    tok_order = (
        ((tok_index // Z - steps) % Z * Z)[:, None] + ((tok_index % Z - steps) % Z)[None, :]
    ).reshape(-1).astype(jnp.int32)
    own = cache_kv[:, 0]
    other = exchange(own)
    weights = lax.all_gather(
        jnp.concatenate([w_out, beside(w_gate, w_up), w_down.T], axis=1),
        "tok", axis=0, tiled=True,
    )
    cosine, sine = angles_of(cached_len)
    src = sources()
    att_0, qt_1, kv_1, cache_new, rows = attend_first(
        cached_len, part_index.reshape(1), src, tok_order, attn_gain[None], cosine, sine,
        x_pieces, w_pieces, own, other,
    )
    pieces_0 = gather_head(att_0)
    att_1 = attend_second(cached_len, qt_1, kv_1)
    pieces_1 = gather_head(att_1)
    gain = mlp_gain[None]
    residual_0, normed_0 = project_out(src, gain, weights, rows, pieces_0, 0)
    residual_1, normed_1 = project_out(src, gain, weights, rows, pieces_1, 1)
    half_count = head_count // 2
    low = normed_0.reshape(half_count, row_count, width)
    high = normed_1.reshape(half_count, row_count, width)
    residual = lax.dynamic_index_in_dim(
        jnp.concatenate([residual_0, residual_1]).reshape(head_count, row_count, width),
        head_index, 0, keepdims=False,
    )
    z = head_index // 2
    core = (head_index % 2).reshape(1)
    outs = []
    for chunk in range(2):
        mine, theirs = feed_forward(core, low, high, weights, chunk, w_out.shape[1], units)
        pair = (mine.astype(jnp.float32) + exchange(theirs).astype(jnp.float32)).astype(
            jnp.bfloat16
        )
        rows_here = row_count // 2
        total = residual[chunk * rows_here : (chunk + 1) * rows_here].astype(jnp.float32)
        total = total + lax.dynamic_index_in_dim(pair, z, 0, keepdims=False).astype(jnp.float32)
        for d in range(1, Z):
            sent = lax.dynamic_index_in_dim(pair, (z + d) % Z, 0, keepdims=False)
            total = total + along_z(sent, d).astype(jnp.float32)
        outs.append(total.astype(jnp.bfloat16))
    return (jnp.concatenate(outs), cache_new[:, None])


def solution(mesh):
    return jax.shard_map(
        per_device,
        mesh=mesh,
        in_specs=(
            P(("tok", "head"), None),
            P(),
            P("tok", None),
            P("tok", None),
            P(),
            P("tok", "head"),
            P("tok", "head"),
            P("head", "tok"),
            P("tok", "head", None, None),
            P("tok"),
        ),
        out_specs=(P(("tok", "head"), None), P("tok", "head", None, None)),
        check_vma=False,
    )
```

time: 415 us -> 292 us (0.70)
  the two profiles are of different devices: /device:TPU:0 before, /device:TPU:18 now
where the time goes in v2:
time: 292 us; the launch traced here: 287 us
  Pallas kernels  124 us (42%)
  starting transfers between devices  56.7 us (19%)
  waiting for transfers between devices  53.9 us (18%)
  local copies, waits for them, and re-layouts  29.7 us (10%)
  between operations  14.7 us (5%)
  other arithmetic  7.72 us (3%)
    pallas_call x1, Pallas kernels, attend_first(): pl.pallas_call(first_kernel, out_shape=(jax.ShapeDtypeStruct((S_NEW, head...  45.1 us
    pallas_call x1, Pallas kernels, attend_second(): pl.pallas_call(second_kernel, out_shape=jax.ShapeDtypeStruct((S_NEW, head...  33.4 us
    ppermute x15, starting transfers between devices, along_z(): lax.ppermute(array, 'head', [(i, (i + 2 * distance) % count) for i in ran...  32.9 us
    ppermute x15, waiting for transfers between devices, along_z(): lax.ppermute(array, 'head', [(i, (i + 2 * distance) % count) for i in ran...  29.8 us
    pallas_call x2, Pallas kernels, feed_forward(): pl.pallas_call(kernel, out_shape=(jax.ShapeDtypeStruct((Z, rows, width),...  27.4 us
    ppermute x6, waiting for transfers between devices, along_tok(): return lax.ppermute(array, 'tok', moves)  22.7 us
    unnamed x80, local copies, waits for them, and re-layouts  21.6 us
    ppermute x6, starting transfers between devices, along_tok(): return lax.ppermute(array, 'tok', moves)  19.9 us
  transfers between devices with their start and end apart: 37, of which 17 were waited for; matrix products, arithmetic and copies ran while one was open for 3% of the time, Pallas kernels for 35%

profile of v2, /device:TPU:18, one launch (start us, length us, event | category | flops | bytes accessed | tf_op | source)
XLA Modules:
  0.0 286.7 jit_solution(6961152284169041495)
XLA Ops:
  13.1 2.3 concatenate.16
  20.5 2.1 collective-permute-done.7
  22.6 2.5 collective-permute-done.8
  29.3 1.9 collective-permute-start
  31.3 3.6 %collective-permute-start.1 = (bf16[128,2048]{1,0:T(8,128)(2,1)S(1)}, bf16[128,2048]{1,0:T(8,128)(2,1)}, u32[]{:S(2)}, u32[]{:S(2)}) collective-permute-start(bf16[128,2048]{1,0:T(8,128)(2,1)S(1)} %copy-done.28), channel_id=1, source_target_pairs={{0,4},{1,5},{2,6},{3,7},{4,0},{5,1},{6,2},{7,3},{8,12},{9,13},{10,... | collective-permute-start | bytes 1572872 | tf_op jit(solution)/shard_map/ppermute | solution.py:40
  34.8 12.1 %collective-permute-done.10.refs_9_ = bf16[4,128,384]{2,1,0:T(8,128)(2,1)} collective-permute-done((bf16[4,128,384]{2,1,0:T(8,128)(2,1)S(1)}, bf16[4,128,384]{2,1,0:T(8,128)(2,1)}, u32[]{:S(2)}, u32[]{:S(2)}) %collective-permute-start.10) | collective-permute-done | bytes 393248 | tf_op jit(solution)/shard_map/ppermute | solution.py:48
  46.9 4.1 %collective-permute-start.2 = (bf16[128,2048]{1,0:T(8,128)(2,1)S(1)}, bf16[128,2048]{1,0:T(8,128)(2,1)}, u32[]{:S(2)}, u32[]{:S(2)}) collective-permute-start(bf16[128,2048]{1,0:T(8,128)(2,1)S(1)} %copy-done.28), channel_id=1, source_target_pairs={{0,6},{1,7},{2,0},{3,1},{4,2},{5,3},{6,4},{7,5},{8,14},{9,15},{10,... | collective-permute-start | bytes 1572872 | tf_op jit(solution)/shard_map/ppermute | solution.py:40
  51.0 14.2 %collective-permute-start.12 = (bf16[4,128,384]{2,1,0:T(8,128)(2,1)S(1)}, bf16[4,128,384]{2,1,0:T(8,128)(2,1)}, u32[]{:S(2)}, u32[]{:S(2)}) collective-permute-start(bf16[4,128,384]{2,1,0:T(8,128)(2,1)S(1)} %pad_maximum_fusion.2.refs_8_), channel_id=1, source_target_pairs={{0,96},{8,104},{16,112},{24,120},{32,0},{40,8},{48,16},{56,24},{64... | collective-permute-start | bytes 1179656 | tf_op jit(solution)/shard_map/ppermute | solution.py:48
  66.0 4.5 %collective-permute-done.12.refs_11_ = bf16[4,128,384]{2,1,0:T(8,128)(2,1)} collective-permute-done((bf16[4,128,384]{2,1,0:T(8,128)(2,1)S(1)}, bf16[4,128,384]{2,1,0:T(8,128)(2,1)}, u32[]{:S(2)}, u32[]{:S(2)}) %collective-permute-start.12) | collective-permute-done | bytes 393248 | tf_op jit(solution)/shard_map/ppermute | solution.py:48
  75.7 45.1 %attend_first.1 = (bf16[512,256]{1,0:T(8,128)(2,1)}, bf16[4,128,512]{2,1,0:T(8,128)(2,1)}, bf16[8720,128]{1,0:T(8,128)(2,1)}, bf16[2,4352,128]{2,1,0:T(8,128)(2,1)}, bf16[1024,2048]{1,0:T(8,128)(2,1)}) custom-call(s32[2]{0:T(128)} %len_ref.1, s32[1]{0:T(128)} %bitcast.2.part_ref.refs_0_, s32[8]{0:T(128)} %pad_add_fusion.src_ref, s32[16]{0:T(128)} %add.183.tok_ref, ...), custom_call_target="tpu_custom_call" | custom-call | flops 10000000000 | bytes 40000000 | tf_op jit(solution)/shard_map/attend_first/pallas_call | solution.py:240
  120.8 1.6 copy-done.23
  123.4 33.4 %attend_second.1.refs_0_ = bf16[512,256]{1,0:T(8,128)(2,1)S(1)} custom-call(s32[2]{0:T(128)S(1)} %copy-done.22, bf16[4,128,512]{2,1,0:T(8,128)(2,1)S(1)} %copy-done.24, bf16[8720,128]{1,0:T(8,128)(2,1)S(1)} %copy-done.23), custom_call_target="tpu_custom_call" | custom-call | flops 10000000000 | bytes 40000000 | tf_op jit(solution)/shard_map/attend_second/pallas_call | solution.py:279
  156.9 2.2 collective-permute-start.21
  159.0 5.6 %collective-permute-start.22 = (bf16[512,256]{1,0:T(8,128)(2,1)S(1)}, bf16[512,256]{1,0:T(8,128)(2,1)S(1)}, u32[]{:S(2)}, u32[]{:S(2)}) collective-permute-start(bf16[512,256]{1,0:T(8,128)(2,1)S(1)} %attend_second.1.refs_0_), channel_id=1, source_target_pairs={{0,4},{1,5},{2,6},{3,7},{4,0},{5,1},{6,2},{7,3},{8,12},{9,13},{10,... | collective-permute-start | bytes 786440 | tf_op jit(solution)/shard_map/ppermute | solution.py:40
  164.8 1.9 collective-permute-start.14
  166.7 3.6 %collective-permute-done.21.refs_1_ = bf16[512,256]{1,0:T(8,128)(2,1)S(1)} collective-permute-done((bf16[512,256]{1,0:T(8,128)(2,1)S(1)}, bf16[512,256]{1,0:T(8,128)(2,1)S(1)}, u32[]{:S(2)}, u32[]{:S(2)}) %collective-permute-start.21) | collective-permute-done | bytes 262176 | tf_op jit(solution)/shard_map/ppermute | solution.py:40
  170.3 6.6 %collective-permute-start.15 = (bf16[512,256]{1,0:T(8,128)(2,1)S(1)}, bf16[512,256]{1,0:T(8,128)(2,1)S(1)}, u32[]{:S(2)}, u32[]{:S(2)}) collective-permute-start(bf16[512,256]{1,0:T(8,128)(2,1)S(1)} %copy-done.6), channel_id=1, source_target_pairs={{0,4},{1,5},{2,6},{3,7},{4,0},{5,1},{6,2},{7,3},{8,12},{9,13},{10,... | collective-permute-start | bytes 786440 | tf_op jit(solution)/shard_map/ppermute | solution.py:40
  179.3 1.7 collective-permute-done.14.refs_1_
  181.8 6.1 %collective-permute-done.15.refs_2_ = bf16[512,256]{1,0:T(8,128)(2,1)S(1)} collective-permute-done((bf16[512,256]{1,0:T(8,128)(2,1)S(1)}, bf16[512,256]{1,0:T(8,128)(2,1)S(1)}, u32[]{:S(2)}, u32[]{:S(2)}) %collective-permute-start.15) | collective-permute-done | bytes 262176 | tf_op jit(solution)/shard_map/ppermute | solution.py:40
  191.4 2.2 copy-done
  199.3 8.5 %project_out.3 = (bf16[512,2048]{1,0:T(8,128)(2,1)S(1)}, bf16[512,2048]{1,0:T(8,128)(2,1)S(1)}) custom-call(s32[8]{0:T(128)S(1)} %copy-done.20, f32[1,2048]{1,0:T(1,128)S(1)} %bitcast.51, bf16[2048,4160]{1,0:T(8,128)(2,1)} %all-gather.2.cloned.1.call-done.w_ref.refs_3_, bf16[1024,2048]{1,0:T(8,128)(2,1)S(1)} %copy-done, ...), custom_call_target="tpu_custom_call" | custom-call | flops 4000000000 | bytes 20000000 | tf_op jit(solution)/shard_map/project_out/pallas_call | solution.py:331
  209.1 9.6 %project_out.2 = (bf16[512,2048]{1,0:T(8,128)(2,1)S(1)}, bf16[512,2048]{1,0:T(8,128)(2,1)S(1)}) custom-call(s32[8]{0:T(128)S(1)} %copy-done.20, f32[1,2048]{1,0:T(1,128)S(1)} %bitcast.52, bf16[2048,4160]{1,0:T(8,128)(2,1)} %all-gather.2.cloned.1.call-done.w_ref.refs_3_, bf16[1024,2048]{1,0:T(8,128)(2,1)S(1)} %copy-done.1, bf16[512,256]{1,0:T(8,128)(2,1)S(1)} %copy-done.6, ...), custom_call_target="tpu_custom_call" | custom-call | flops 4000000000 | bytes 20000000 | tf_op jit(solution)/shard_map/project_out/pallas_call | solution.py:331
  220.1 13.7 %feed_forward.3 = (bf16[4,64,2048]{2,1,0:T(8,128)(2,1)S(1)}, bf16[4,64,2048]{2,1,0:T(8,128)(2,1)}) custom-call(s32[1]{0:T(128)} %bitcast.2.part_ref.refs_0_, bf16[4,128,2048]{2,1,0:T(8,128)(2,1)S(1)} %bitcast.49, bf16[4,128,2048]{2,1,0:T(8,128)(2,1)} %bitcast.47, bf16[2048,4160]{1,0:T(8,128)(2,1)} %all-gather.2.cloned.1.call-done.w_ref.refs_3_), custom_call_target="tpu_custom_call" | custom-call | flops 5000000000 | bytes 16000000 | tf_op jit(solution)/shard_map/feed_forward/pallas_call | solution.py:416
  234.9 13.7 %feed_forward.2 = (bf16[4,64,2048]{2,1,0:T(8,128)(2,1)S(1)}, bf16[4,64,2048]{2,1,0:T(8,128)(2,1)}) custom-call(s32[1]{0:T(128)} %bitcast.2.part_ref.refs_0_, bf16[4,128,2048]{2,1,0:T(8,128)(2,1)S(1)} %bitcast.50, bf16[4,128,2048]{2,1,0:T(8,128)(2,1)} %bitcast.48, bf16[2048,4160]{1,0:T(8,128)(2,1)} %all-gather.2.cloned.1.call-done.w_ref.refs_3_), custom_call_target="tpu_custom_call" | custom-call | flops 5000000000 | bytes 16000000 | tf_op jit(solution)/shard_map/feed_forward/pallas_call | solution.py:416
  249.2 1.9 add_convert_fusion
  251.6 3.0 %collective-permute-start.34 = (bf16[64,2048]{1,0:T(8,128)(2,1)S(1)}, bf16[64,2048]{1,0:T(8,128)(2,1)S(1)}, u32[]{:S(2)}, u32[]{:S(2)}) collective-permute-start(bf16[64,2048]{1,0:T(8,128)(2,1)S(1)} %get-tuple-element.37), channel_id=1, source_target_pairs={{0,4},{1,5},{2,6},{3,7},{4,0},{5,1},{6,2},{7,3},{8,12},{9,13},{10,... | collective-permute-start | bytes 786440 | tf_op jit(solution)/shard_map/ppermute | solution.py:40
  254.9 1.8 add_convert_fusion.1
  256.8 1.7 collective-permute-start.29
  259.5 2.3 collective-permute-done.33
  262.8 4.6 %collective-permute-done.34 = bf16[64,2048]{1,0:T(8,128)(2,1)S(1)} collective-permute-done((bf16[64,2048]{1,0:T(8,128)(2,1)S(1)}, bf16[64,2048]{1,0:T(8,128)(2,1)S(1)}, u32[]{:S(2)}, u32[]{:S(2)}) %collective-permute-start.34) | collective-permute-done | bytes 262176 | tf_op jit(solution)/shard_map/ppermute | solution.py:40
  268.2 3.8 %collective-permute-done.29 = bf16[64,2048]{1,0:T(8,128)(2,1)S(1)} collective-permute-done((bf16[64,2048]{1,0:T(8,128)(2,1)S(1)}, bf16[64,2048]{1,0:T(8,128)(2,1)S(1)}, u32[]{:S(2)}, u32[]{:S(2)}) %collective-permute-start.29) | collective-permute-done | bytes 262176 | tf_op jit(solution)/shard_map/ppermute | solution.py:40
  272.0 6.0 %collective-permute-done.30 = bf16[64,2048]{1,0:T(8,128)(2,1)S(1)} collective-permute-done((bf16[64,2048]{1,0:T(8,128)(2,1)S(1)}, bf16[64,2048]{1,0:T(8,128)(2,1)S(1)}, u32[]{:S(2)}, u32[]{:S(2)}) %collective-permute-start.30) | collective-permute-done | bytes 262176 | tf_op jit(solution)/shard_map/ppermute | solution.py:40
  (154 shorter events, 44.0 us)
Async XLA Ops:
  7.2 184.2 %all-gather.2.cloned.1.call-start = ((), (), s32[]{:S(2)}) async-start(), calls=%async_computation | async-start | bytes 18382848 | tf_op jit(solution)/shard_map/all_gather | solution.py:485
  15.5 59.4 %collective-permute-start.13 = (bf16[2,4352,128]{2,1,0:T(8,128)(2,1)S(1)}, bf16[2,4352,128]{2,1,0:T(8,128)(2,1)}, u32[]{:S(2)}, u32[]{:S(2)}) collective-permute-start(bf16[2,4352,128]{2,1,0:T(8,128)(2,1)S(1)} %bitcast.60), channel_id=1, source_target_pairs={{0,1},{1,0},{2,3},{3,2},{4,5},{5,4},{6,7},{7,6},{8,9},{9,8},{10,11... | collective-permute-start | bytes 6684680 | tf_op jit(solution)/shard_map/ppermute | solution.py:35
  18.8 6.4 %collective-permute-start.8 = (bf16[128,384]{1,0:T(8,128)(2,1)S(1)}, bf16[128,384]{1,0:T(8,128)(2,1)S(1)}, u32[]{:S(2)}, u32[]{:S(2)}) collective-permute-start(bf16[128,384]{1,0:T(8,128)(2,1)S(1)} %pad_maximum_fusion.3), channel_id=1, source_target_pairs={{0,16},{8,24},{16,0},{24,8},{32,48},{40,56},{48,32},{56,40},{64,80... | collective-permute-start | bytes 294920 | tf_op jit(solution)/shard_map/ppermute | solution.py:48
  19.4 7.2 %collective-permute-start.9 = (bf16[128,384]{1,0:T(8,128)(2,1)S(1)}, bf16[128,384]{1,0:T(8,128)(2,1)S(1)}, u32[]{:S(2)}, u32[]{:S(2)}) collective-permute-start(bf16[128,384]{1,0:T(8,128)(2,1)S(1)} %pad_maximum_fusion.3), channel_id=1, source_target_pairs={{0,24},{8,0},{16,8},{24,16},{32,56},{40,32},{48,40},{56,48},{64,88... | collective-permute-start | bytes 294920 | tf_op jit(solution)/shard_map/ppermute | solution.py:48
  26.7 20.2 %collective-permute-start.10 = (bf16[4,128,384]{2,1,0:T(8,128)(2,1)S(1)}, bf16[4,128,384]{2,1,0:T(8,128)(2,1)}, u32[]{:S(2)}, u32[]{:S(2)}) collective-permute-start(bf16[4,128,384]{2,1,0:T(8,128)(2,1)S(1)} %pad_maximum_fusion.2.refs_8_), channel_id=1, source_target_pairs={{0,32},{8,40},{16,48},{24,56},{32,64},{40,72},{48,80},{56,88},{64,... | collective-permute-start | bytes 1179656 | tf_op jit(solution)/shard_map/ppermute | solution.py:48
  28.2 22.8 %collective-permute-start.11 = (bf16[4,128,384]{2,1,0:T(8,128)(2,1)S(1)}, bf16[4,128,384]{2,1,0:T(8,128)(2,1)}, u32[]{:S(2)}, u32[]{:S(2)}) collective-permute-start(bf16[4,128,384]{2,1,0:T(8,128)(2,1)S(1)} %pad_maximum_fusion.2.refs_8_), channel_id=1, source_target_pairs={{0,64},{8,72},{16,80},{24,88},{32,96},{40,104},{48,112},{56,120},{... | collective-permute-start | bytes 1179656 | tf_op jit(solution)/shard_map/ppermute | solution.py:48
  29.3 41.2 %collective-permute-start = (bf16[128,2048]{1,0:T(8,128)(2,1)S(1)}, bf16[128,2048]{1,0:T(8,128)(2,1)}, u32[]{:S(2)}, u32[]{:S(2)}) collective-permute-start(bf16[128,2048]{1,0:T(8,128)(2,1)S(1)} %copy-done.28), channel_id=1, source_target_pairs={{0,2},{1,3},{2,4},{3,5},{4,6},{5,7},{6,0},{7,1},{8,10},{9,11},{10,... | collective-permute-start | bytes 1572872 | tf_op jit(solution)/shard_map/ppermute | solution.py:40
  31.3 39.8 %collective-permute-start.1 = (bf16[128,2048]{1,0:T(8,128)(2,1)S(1)}, bf16[128,2048]{1,0:T(8,128)(2,1)}, u32[]{:S(2)}, u32[]{:S(2)}) collective-permute-start(bf16[128,2048]{1,0:T(8,128)(2,1)S(1)} %copy-done.28), channel_id=1, source_target_pairs={{0,4},{1,5},{2,6},{3,7},{4,0},{5,1},{6,2},{7,3},{8,12},{9,13},{10,... | collective-permute-start | bytes 1572872 | tf_op jit(solution)/shard_map/ppermute | solution.py:40
  46.9 24.2 %collective-permute-start.2 = (bf16[128,2048]{1,0:T(8,128)(2,1)S(1)}, bf16[128,2048]{1,0:T(8,128)(2,1)}, u32[]{:S(2)}, u32[]{:S(2)}) collective-permute-start(bf16[128,2048]{1,0:T(8,128)(2,1)S(1)} %copy-done.28), channel_id=1, source_target_pairs={{0,6},{1,7},{2,0},{3,1},{4,2},{5,3},{6,4},{7,5},{8,14},{9,15},{10,... | collective-permute-start | bytes 1572872 | tf_op jit(solution)/shard_map/ppermute | solution.py:40
  51.0 19.5 %collective-permute-start.12 = (bf16[4,128,384]{2,1,0:T(8,128)(2,1)S(1)}, bf16[4,128,384]{2,1,0:T(8,128)(2,1)}, u32[]{:S(2)}, u32[]{:S(2)}) collective-permute-start(bf16[4,128,384]{2,1,0:T(8,128)(2,1)S(1)} %pad_maximum_fusion.2.refs_8_), channel_id=1, source_target_pairs={{0,96},{8,104},{16,112},{24,120},{32,0},{40,8},{48,16},{56,24},{64... | collective-permute-start | bytes 1179656 | tf_op jit(solution)/shard_map/ppermute | solution.py:48
  156.9 13.4 %collective-permute-start.21 = (bf16[512,256]{1,0:T(8,128)(2,1)S(1)}, bf16[512,256]{1,0:T(8,128)(2,1)S(1)}, u32[]{:S(2)}, u32[]{:S(2)}) collective-permute-start(bf16[512,256]{1,0:T(8,128)(2,1)S(1)} %attend_second.1.refs_0_), channel_id=1, source_target_pairs={{0,2},{1,3},{2,4},{3,5},{4,6},{5,7},{6,0},{7,1},{8,10},{9,11},{10,... | collective-permute-start | bytes 786440 | tf_op jit(solution)/shard_map/ppermute | solution.py:40
  159.0 18.4 %collective-permute-start.22 = (bf16[512,256]{1,0:T(8,128)(2,1)S(1)}, bf16[512,256]{1,0:T(8,128)(2,1)S(1)}, u32[]{:S(2)}, u32[]{:S(2)}) collective-permute-start(bf16[512,256]{1,0:T(8,128)(2,1)S(1)} %attend_second.1.refs_0_), channel_id=1, source_target_pairs={{0,4},{1,5},{2,6},{3,7},{4,0},{5,1},{6,2},{7,3},{8,12},{9,13},{10,... | collective-permute-start | bytes 786440 | tf_op jit(solution)/shard_map/ppermute | solution.py:40
  164.6 12.8 %collective-permute-start.23 = (bf16[512,256]{1,0:T(8,128)(2,1)S(1)}, bf16[512,256]{1,0:T(8,128)(2,1)S(1)}, u32[]{:S(2)}, u32[]{:S(2)}) collective-permute-start(bf16[512,256]{1,0:T(8,128)(2,1)S(1)} %attend_second.1.refs_0_), channel_id=1, source_target_pairs={{0,6},{1,7},{2,0},{3,1},{4,2},{5,3},{6,4},{7,5},{8,14},{9,15},{10,... | collective-permute-start | bytes 786440 | tf_op jit(solution)/shard_map/ppermute | solution.py:40
  164.8 12.7 %collective-permute-start.24 = (bf16[512,256]{1,0:T(8,128)(2,1)S(1)}, bf16[512,256]{1,0:T(8,128)(2,1)S(1)}, u32[]{:S(2)}, u32[]{:S(2)}) collective-permute-start(bf16[512,256]{1,0:T(8,128)(2,1)S(1)} %attend_second.1.refs_0_), channel_id=1, source_target_pairs={{0,1},{1,0},{2,3},{3,2},{4,5},{5,4},{6,7},{7,6},{8,9},{9,8},{10,11... | collective-permute-start | bytes 786440 | tf_op jit(solution)/shard_map/ppermute | solution.py:35
  164.8 16.3 %collective-permute-start.14 = (bf16[512,256]{1,0:T(8,128)(2,1)S(1)}, bf16[512,256]{1,0:T(8,128)(2,1)S(1)}, u32[]{:S(2)}, u32[]{:S(2)}) collective-permute-start(bf16[512,256]{1,0:T(8,128)(2,1)S(1)} %copy-done.6), channel_id=1, source_target_pairs={{0,2},{1,3},{2,4},{3,5},{4,6},{5,7},{6,0},{7,1},{8,10},{9,11},{10,... | collective-permute-start | bytes 786440 | tf_op jit(solution)/shard_map/ppermute | solution.py:40
  170.3 17.6 %collective-permute-start.15 = (bf16[512,256]{1,0:T(8,128)(2,1)S(1)}, bf16[512,256]{1,0:T(8,128)(2,1)S(1)}, u32[]{:S(2)}, u32[]{:S(2)}) collective-permute-start(bf16[512,256]{1,0:T(8,128)(2,1)S(1)} %copy-done.6), channel_id=1, source_target_pairs={{0,4},{1,5},{2,6},{3,7},{4,0},{5,1},{6,2},{7,3},{8,12},{9,13},{10,... | collective-permute-start | bytes 786440 | tf_op jit(solution)/shard_map/ppermute | solution.py:40
  177.4 10.5 %collective-permute-start.16 = (bf16[512,256]{1,0:T(8,128)(2,1)S(1)}, bf16[512,256]{1,0:T(8,128)(2,1)}, u32[]{:S(2)}, u32[]{:S(2)}) collective-permute-start(bf16[512,256]{1,0:T(8,128)(2,1)S(1)} %copy-done.6), channel_id=1, source_target_pairs={{0,6},{1,7},{2,0},{3,1},{4,2},{5,3},{6,4},{7,5},{8,14},{9,15},{10,... | collective-permute-start | bytes 786440 | tf_op jit(solution)/shard_map/ppermute | solution.py:40
  177.4 11.0 %collective-permute-start.25 = (bf16[512,256]{1,0:T(8,128)(2,1)S(1)}, bf16[512,256]{1,0:T(8,128)(2,1)S(1)}, u32[]{:S(2)}, u32[]{:S(2)}) collective-permute-start(bf16[512,256]{1,0:T(8,128)(2,1)S(1)} %collective-permute-done.21.refs_1_), channel_id=1, source_target_pairs={{0,1},{1,0},{2,3},{3,2},{4,5},{5,4},{6,7},{7,6},{8,9},{9,8},{10,11... | collective-permute-start | bytes 786440 | tf_op jit(solution)/shard_map/ppermute | solution.py:35
  178.1 11.0 %collective-permute-start.26 = (bf16[512,256]{1,0:T(8,128)(2,1)S(1)}, bf16[512,256]{1,0:T(8,128)(2,1)S(1)}, u32[]{:S(2)}, u32[]{:S(2)}) collective-permute-start(bf16[512,256]{1,0:T(8,128)(2,1)S(1)} %collective-permute-done.22.refs_2_), channel_id=1, source_target_pairs={{0,1},{1,0},{2,3},{3,2},{4,5},{5,4},{6,7},{7,6},{8,9},{9,8},{10,11... | collective-permute-start | bytes 786440 | tf_op jit(solution)/shard_map/ppermute | solution.py:35
  181.1 9.6 %collective-permute-start.27 = (bf16[512,256]{1,0:T(8,128)(2,1)S(1)}, bf16[512,256]{1,0:T(8,128)(2,1)S(1)}, u32[]{:S(2)}, u32[]{:S(2)}) collective-permute-start(bf16[512,256]{1,0:T(8,128)(2,1)S(1)} %collective-permute-done.23.refs_3_), channel_id=1, source_target_pairs={{0,1},{1,0},{2,3},{3,2},{4,5},{5,4},{6,7},{7,6},{8,9},{9,8},{10,11... | collective-permute-start | bytes 786440 | tf_op jit(solution)/shard_map/ppermute | solution.py:35
  187.9 21.2 %collective-permute-start.17 = (bf16[512,256]{1,0:T(8,128)(2,1)S(1)}, bf16[512,256]{1,0:T(8,128)(2,1)}, u32[]{:S(2)}, u32[]{:S(2)}) collective-permute-start(bf16[512,256]{1,0:T(8,128)(2,1)S(1)} %copy-done.6), channel_id=1, source_target_pairs={{0,1},{1,0},{2,3},{3,2},{4,5},{5,4},{6,7},{7,6},{8,9},{9,8},{10,11... | collective-permute-start | bytes 786440 | tf_op jit(solution)/shard_map/ppermute | solution.py:35
  187.9 21.2 %collective-permute-start.18 = (bf16[512,256]{1,0:T(8,128)(2,1)S(1)}, bf16[512,256]{1,0:T(8,128)(2,1)}, u32[]{:S(2)}, u32[]{:S(2)}) collective-permute-start(bf16[512,256]{1,0:T(8,128)(2,1)S(1)} %collective-permute-done.14.refs_1_), channel_id=1, source_target_pairs={{0,1},{1,0},{2,3},{3,2},{4,5},{5,4},{6,7},{7,6},{8,9},{9,8},{10,11... | collective-permute-start | bytes 786440 | tf_op jit(solution)/shard_map/ppermute | solution.py:35
  189.1 20.0 %collective-permute-start.19 = (bf16[512,256]{1,0:T(8,128)(2,1)S(1)}, bf16[512,256]{1,0:T(8,128)(2,1)}, u32[]{:S(2)}, u32[]{:S(2)}) collective-permute-start(bf16[512,256]{1,0:T(8,128)(2,1)S(1)} %collective-permute-done.15.refs_2_), channel_id=1, source_target_pairs={{0,1},{1,0},{2,3},{3,2},{4,5},{5,4},{6,7},{7,6},{8,9},{9,8},{10,11... | collective-permute-start | bytes 786440 | tf_op jit(solution)/shard_map/ppermute | solution.py:35
  189.8 19.3 %collective-permute-start.20 = (bf16[512,256]{1,0:T(8,128)(2,1)}, bf16[512,256]{1,0:T(8,128)(2,1)}, u32[]{:S(2)}, u32[]{:S(2)}) collective-permute-start(bf16[512,256]{1,0:T(8,128)(2,1)} %collective-permute-done.16.refs_3_), channel_id=1, source_target_pairs={{0,1},{1,0},{2,3},{3,2},{4,5},{5,4},{6,7},{7,6},{8,9},{9,8},{10,11... | collective-permute-start | bytes 786440 | tf_op jit(solution)/shard_map/ppermute | solution.py:35
  234.8 14.4 %collective-permute-start.32 = (bf16[4,64,2048]{2,1,0:T(8,128)(2,1)}, bf16[4,64,2048]{2,1,0:T(8,128)(2,1)}, u32[]{:S(2)}, u32[]{:S(2)}) collective-permute-start(bf16[4,64,2048]{2,1,0:T(8,128)(2,1)} %get-tuple-element.26), channel_id=1, source_target_pairs={{0,1},{1,0},{2,3},{3,2},{4,5},{5,4},{6,7},{7,6},{8,9},{9,8},{10,11... | collective-permute-start | bytes 3145736 | tf_op jit(solution)/shard_map/ppermute | solution.py:35
  248.6 6.3 %collective-permute-start.28 = (bf16[4,64,2048]{2,1,0:T(8,128)(2,1)}, bf16[4,64,2048]{2,1,0:T(8,128)(2,1)}, u32[]{:S(2)}, u32[]{:S(2)}) collective-permute-start(bf16[4,64,2048]{2,1,0:T(8,128)(2,1)} %get-tuple-element.24), channel_id=1, source_target_pairs={{0,1},{1,0},{2,3},{3,2},{4,5},{5,4},{6,7},{7,6},{8,9},{9,8},{10,11... | collective-permute-start | bytes 3145736 | tf_op jit(solution)/shard_map/ppermute | solution.py:35
  251.2 10.5 %collective-permute-start.33 = (bf16[64,2048]{1,0:T(8,128)(2,1)S(1)}, bf16[64,2048]{1,0:T(8,128)(2,1)S(1)}, u32[]{:S(2)}, u32[]{:S(2)}) collective-permute-start(bf16[64,2048]{1,0:T(8,128)(2,1)S(1)} %get-tuple-element.35), channel_id=1, source_target_pairs={{0,2},{1,3},{2,4},{3,5},{4,6},{5,7},{6,0},{7,1},{8,10},{9,11},{10,... | collective-permute-start | bytes 786440 | tf_op jit(solution)/shard_map/ppermute | solution.py:40
  251.6 15.7 %collective-permute-start.34 = (bf16[64,2048]{1,0:T(8,128)(2,1)S(1)}, bf16[64,2048]{1,0:T(8,128)(2,1)S(1)}, u32[]{:S(2)}, u32[]{:S(2)}) collective-permute-start(bf16[64,2048]{1,0:T(8,128)(2,1)S(1)} %get-tuple-element.37), channel_id=1, source_target_pairs={{0,4},{1,5},{2,6},{3,7},{4,0},{5,1},{6,2},{7,3},{8,12},{9,13},{10,... | collective-permute-start | bytes 786440 | tf_op jit(solution)/shard_map/ppermute | solution.py:40
  254.6 13.6 %collective-permute-start.35 = (bf16[64,2048]{1,0:T(8,128)(2,1)S(1)}, bf16[64,2048]{1,0:T(8,128)(2,1)S(1)}, u32[]{:S(2)}, u32[]{:S(2)}) collective-permute-start(bf16[64,2048]{1,0:T(8,128)(2,1)S(1)} %get-tuple-element.36), channel_id=1, source_target_pairs={{0,6},{1,7},{2,0},{3,1},{4,2},{5,3},{6,4},{7,5},{8,14},{9,15},{10,... | collective-permute-start | bytes 786440 | tf_op jit(solution)/shard_map/ppermute | solution.py:40
  256.8 15.2 %collective-permute-start.29 = (bf16[64,2048]{1,0:T(8,128)(2,1)S(1)}, bf16[64,2048]{1,0:T(8,128)(2,1)S(1)}, u32[]{:S(2)}, u32[]{:S(2)}) collective-permute-start(bf16[64,2048]{1,0:T(8,128)(2,1)S(1)} %get-tuple-element.32), channel_id=1, source_target_pairs={{0,2},{1,3},{2,4},{3,5},{4,6},{5,7},{6,0},{7,1},{8,10},{9,11},{10,... | collective-permute-start | bytes 786440 | tf_op jit(solution)/shard_map/ppermute | solution.py:40
  258.5 19.6 %collective-permute-start.30 = (bf16[64,2048]{1,0:T(8,128)(2,1)S(1)}, bf16[64,2048]{1,0:T(8,128)(2,1)S(1)}, u32[]{:S(2)}, u32[]{:S(2)}) collective-permute-start(bf16[64,2048]{1,0:T(8,128)(2,1)S(1)} %get-tuple-element.34), channel_id=1, source_target_pairs={{0,4},{1,5},{2,6},{3,7},{4,0},{5,1},{6,2},{7,3},{8,12},{9,13},{10,... | collective-permute-start | bytes 786440 | tf_op jit(solution)/shard_map/ppermute | solution.py:40
  261.7 16.6 %collective-permute-start.31 = (bf16[64,2048]{1,0:T(8,128)(2,1)S(1)}, bf16[64,2048]{1,0:T(8,128)(2,1)S(1)}, u32[]{:S(2)}, u32[]{:S(2)}) collective-permute-start(bf16[64,2048]{1,0:T(8,128)(2,1)S(1)} %get-tuple-element.33), channel_id=1, source_target_pairs={{0,6},{1,7},{2,0},{3,1},{4,2},{5,3},{6,4},{7,5},{8,14},{9,15},{10,... | collective-permute-start | bytes 786440 | tf_op jit(solution)/shard_map/ppermute | solution.py:40
  (38 other events, 406.9 us)
Sparse Core Ops, SparseCore 0:
  15.6 129.9 all-gather.1
